TPU v7x, 32 devices: a whole 2x2x4 slice. The times are simulated.
32 devices in a mesh: row: 4 (over z), col: 8 (over y, x, core).
Axes of the slice: x: 2, y: 2, z: 4, core: 2. Of those that a mesh axis runs over, the one named last changes fastest.
Arguments:
- tokens: bfloat16 [192, 384, 256], P('row', 'col'), may hold values from -6 to 6
- registers: bfloat16 [64, 256], replicated, may hold values from -6 to 6
- tile_mask: int32 [24, 48], P('row', 'col'), may hold values 0 or 1
- w_qkv: bfloat16 [2, 256, 768], replicated, may hold values from -4 to 4
- w_out: bfloat16 [2, 256, 256], replicated, may hold values from -0.375 to 0.375
- w_up: bfloat16 [2, 256, 1024], replicated, may hold values from -0.375 to 0.375
- w_down: bfloat16 [2, 1024, 256], replicated, may hold values from -0.1875 to 0.1875
- norm_attn: float32 [2, 256], replicated, may hold values from 0.1 to 1.9
- norm_mlp: float32 [2, 256], replicated, may hold values from 0.1 to 1.9
Outputs:
- tokens_out: bfloat16 [192, 384, 256], P('row', 'col')
- registers_out: bfloat16 [64, 256], replicated
All inputs are finite; a program needn't handle non-finite values. No bound on the sum of `tile_mask` on one device may be relied on, other than what follows from the above.
Results may differ from a plain program's by a relative error of at most 0.025.
Values may be sent and summed in bfloat16 or wider, within the bound.
No kernel may reach another device: no remote copies, remote signals or barrier semaphores. Data moves between devices by JAX's collectives and lax.ppermute only.
A program may use at most 128 MiB of HBM per device.

v0:
```python
import math

import jax
import jax.numpy as jnp
from jax import lax
from jax.sharding import PartitionSpec as P

HEADS = 8
LAYERS = 2


neg_large = -1e30
eps_norm = 1e-05
dilation_list = (1, 2)


def extended(block, sides, width):
    for axis, dim in sides:
        count = lax.axis_size(axis)
        forward = [(i, i + 1) for i in range(count - 1)]
        backward = [(target, source) for source, target in forward]
        low = lax.ppermute(
            lax.slice_in_dim(block, block.shape[dim] - width, None, axis=dim), axis, forward
        )
        high = lax.ppermute(lax.slice_in_dim(block, 0, width, axis=dim), axis, backward)
        block = jnp.concatenate([low, block, high], axis=dim)
    return block


def joined(part, axis, combine):
    gathered = jax.tree.map(lambda a: lax.all_gather(a, axis), part)

    def take(source):
        return jax.tree.map(lambda a: lax.dynamic_index_in_dim(a, source, 0, False), gathered)

    return lax.fori_loop(
        1, lax.axis_size(axis), lambda source, state: combine(state, take(source)), take(0)
    )


def layer_norm(x, gain):
    value_rows = x.astype(jnp.float32)
    mean = jnp.mean(value_rows, axis=-1, keepdims=True)
    centred = value_rows - mean
    spread = jnp.mean(centred * centred, axis=-1, keepdims=True)
    return centred * lax.rsqrt(spread + eps_norm) * gain


def window_table():
    query_rows = jnp.arange(64)
    key_rows = jnp.arange(576)
    qrow = (query_rows // 8)[:, None]
    qcol = (query_rows % 8)[:, None]
    krow = (key_rows // 24)[None, :]
    kcol = (key_rows % 24)[None, :]
    return (krow >= qrow) & (krow <= qrow + 12) & (kcol >= qcol) & (kcol <= qcol + 12)


def split_into_tiles(receptive_field, dilation_step):
    grid_rows, grid_columns = (receptive_field.shape[0], receptive_field.shape[1])
    extra_tokens = receptive_field.shape[2:]
    remaining_tokens = tuple(range(len(extra_tokens)))
    row_offset, column_offset = (grid_rows // dilation_step, grid_columns // dilation_step)
    shifted_grid = receptive_field.reshape(
        (row_offset, dilation_step, column_offset, dilation_step) + extra_tokens
    )
    shifted_grid = jnp.transpose(
        shifted_grid, (1, 3, 0, 2) + tuple((4 + token_count for token_count in remaining_tokens))
    )
    shifted_grid = shifted_grid.reshape(
        (dilation_step * dilation_step, row_offset // 8, 8, column_offset // 8, 8) + extra_tokens
    )
    shifted_grid = jnp.transpose(
        shifted_grid, (0, 1, 3, 2, 4) + tuple((5 + token_count for token_count in remaining_tokens))
    )
    return shifted_grid.reshape(
        (dilation_step * dilation_step * (row_offset // 8) * (column_offset // 8), 64)
        + extra_tokens
    )


def untile_grid(grid_tiles, dilation_step, grid_rows, grid_columns):
    window_width = grid_tiles.shape[-1]
    row_offset, column_offset = (grid_rows // dilation_step, grid_columns // dilation_step)
    shifted_grid = grid_tiles.reshape(
        dilation_step, dilation_step, row_offset // 8, column_offset // 8, 8, 8, window_width
    )
    shifted_grid = jnp.transpose(shifted_grid, (2, 4, 0, 3, 5, 1, 6))
    return shifted_grid.reshape(grid_rows, grid_columns, window_width)


def split_into_regions(padded_grid, dilation_step, grid_rows, grid_columns):
    extra_tokens = padded_grid.shape[2:]
    remaining_tokens = tuple(range(len(extra_tokens)))
    padded_grid = jnp.pad(
        padded_grid,
        ((0, 4 * dilation_step), (0, 4 * dilation_step))
        + tuple(((0, 0) for token_count in remaining_tokens)),
    )
    row_padding, column_padding = (
        grid_rows // dilation_step + 16,
        grid_columns // dilation_step + 16,
    )
    shifted_grid = padded_grid.reshape(
        (row_padding, dilation_step, column_padding, dilation_step) + extra_tokens
    )
    shifted_grid = jnp.transpose(
        shifted_grid, (1, 3, 0, 2) + tuple((4 + token_count for token_count in remaining_tokens))
    )
    shifted_grid = shifted_grid.reshape(
        (dilation_step * dilation_step, row_padding // 8, 8, column_padding // 8, 8) + extra_tokens
    )
    shifted_grid = jnp.transpose(
        shifted_grid, (0, 1, 3, 2, 4) + tuple((5 + token_count for token_count in remaining_tokens))
    )
    tile_rows, tile_columns = (grid_rows // dilation_step // 8, grid_columns // dilation_step // 8)
    stacked_outputs = jnp.stack(
        [
            shifted_grid[:, a : a + tile_rows, b : b + tile_columns]
            for a in range(3)
            for b in range(3)
        ],
        axis=3,
    )
    stacked_outputs = stacked_outputs.reshape(
        (dilation_step * dilation_step, tile_rows, tile_columns, 3, 3, 8, 8) + extra_tokens
    )
    stacked_outputs = jnp.transpose(
        stacked_outputs,
        (0, 1, 2, 3, 5, 4, 6) + tuple((7 + token_count for token_count in remaining_tokens)),
    )
    return stacked_outputs.reshape(
        (dilation_step * dilation_step * tile_rows * tile_columns, 576) + extra_tokens
    )


def tile_attention(
    query_rows, key_rows, value_rows, valid_mask, register_keys, register_values, table
):
    group = query_rows.shape[0]
    window_width = query_rows.shape[-1]
    head = window_width // HEADS
    scale = head ** (-0.5)
    q4 = query_rows.reshape(group, 64, HEADS, head)
    k4 = key_rows.reshape(group, 576, HEADS, head)
    v4 = value_rows.reshape(group, 576, HEADS, head)
    rk4 = register_keys.reshape(-1, HEADS, head)
    rv4 = register_values.reshape(-1, HEADS, head)
    near = jnp.einsum("tqhe,tkhe->thqk", q4, k4, preferred_element_type=jnp.float32) * scale
    allowed = table[None, None] & (valid_mask[:, None, None, :] > 0.5)
    near = jnp.where(allowed, near, neg_large)
    far = jnp.einsum("tqhe,rhe->thqr", q4, rk4, preferred_element_type=jnp.float32) * scale
    top = jnp.maximum(jnp.max(near, axis=-1), jnp.max(far, axis=-1))
    near_w = jnp.exp(near - top[..., None])
    far_w = jnp.exp(far - top[..., None])
    total = jnp.sum(near_w, axis=-1) + jnp.sum(far_w, axis=-1)
    out = jnp.einsum(
        "thqk,tkhe->tqhe", near_w.astype(jnp.bfloat16), v4, preferred_element_type=jnp.float32
    )
    out = out + jnp.einsum(
        "thqr,rhe->tqhe", far_w.astype(jnp.bfloat16), rv4, preferred_element_type=jnp.float32
    )
    out = out / jnp.transpose(total, (0, 2, 1))[..., None]
    return out.reshape(group, 64, window_width).astype(jnp.bfloat16)


def gather_neighbour_block(
    query_rows, key_padded, value_padded, mask_padded, register_keys, register_values, dilation_step
):
    grid_rows, grid_columns = (query_rows.shape[0], query_rows.shape[1])
    table = window_table()
    query_tiles = split_into_tiles(query_rows, dilation_step)
    key_tiles = split_into_regions(key_padded, dilation_step, grid_rows, grid_columns)
    value_tiles = split_into_regions(value_padded, dilation_step, grid_rows, grid_columns)
    mask_tiles = split_into_regions(mask_padded, dilation_step, grid_rows, grid_columns)
    count = query_tiles.shape[0]
    group = math.gcd(count, 8)

    def one(pieces):
        return tile_attention(
            pieces[0], pieces[1], pieces[2], pieces[3], register_keys, register_values, table
        )

    output_list = lax.map(
        one,
        (
            query_tiles.reshape((count // group, group) + query_tiles.shape[1:]),
            key_tiles.reshape((count // group, group) + key_tiles.shape[1:]),
            value_tiles.reshape((count // group, group) + value_tiles.shape[1:]),
            mask_tiles.reshape((count // group, group) + mask_tiles.shape[1:]),
        ),
    )
    return untile_grid(
        output_list.reshape(query_tiles.shape), dilation_step, grid_rows, grid_columns
    )


def combine_stats(first, second):
    peak = jnp.maximum(first[0], second[0])
    fa = jnp.exp(first[0] - peak)
    fb = jnp.exp(second[0] - peak)
    head = first[2].shape[1] // HEADS
    return (
        peak,
        first[1] * fa + second[1] * fb,
        first[2] * jnp.repeat(fa, head, axis=1) + second[2] * jnp.repeat(fb, head, axis=1),
    )


def register_partial(reg_q, key_rows, value_rows, live):
    count, window_width = key_rows.shape
    head = window_width // HEADS
    scale = head ** (-0.5)
    rq4 = reg_q.reshape(-1, HEADS, head)
    k4 = key_rows.reshape(count, HEADS, head)
    v4 = value_rows.reshape(count, HEADS, head)
    scores = jnp.einsum("rhe,nhe->rhn", rq4, k4, preferred_element_type=jnp.float32) * scale
    alive = live[None, None, :] > 0.5
    scores = jnp.where(alive, scores, neg_large)
    top = jnp.max(scores, axis=-1)
    weights = jnp.where(alive, jnp.exp(scores - top[..., None]), 0.0)
    total = jnp.sum(weights, axis=-1)
    numer = jnp.einsum(
        "rhn,nhe->rhe", weights.astype(jnp.bfloat16), v4, preferred_element_type=jnp.float32
    )
    return (top, total, numer.reshape(-1, window_width))


def finish_registers(stats, reg_q, register_keys, register_values):
    top, total, numer = stats
    regs, window_width = reg_q.shape
    head = window_width // HEADS
    scale = head ** (-0.5)
    rq4 = reg_q.reshape(regs, HEADS, head)
    rk4 = register_keys.reshape(regs, HEADS, head)
    rv4 = register_values.reshape(regs, HEADS, head)
    own = jnp.einsum("rhe,she->rhs", rq4, rk4, preferred_element_type=jnp.float32) * scale
    own_top = jnp.max(own, axis=-1)
    own_w = jnp.exp(own - own_top[..., None])
    own_total = jnp.sum(own_w, axis=-1)
    own_numer = jnp.einsum(
        "rhs,she->rhe", own_w.astype(jnp.bfloat16), rv4, preferred_element_type=jnp.float32
    )
    peak = jnp.maximum(top, own_top)
    keep = jnp.exp(top - peak)
    keep_own = jnp.exp(own_top - peak)
    total_all = total * keep + own_total * keep_own
    numer_all = numer.reshape(regs, HEADS, head) * keep[..., None] + own_numer * keep_own[..., None]
    return (numer_all / total_all[..., None]).reshape(regs, window_width).astype(jnp.bfloat16)


def extend_rim(value_rows, valid_mask, window_reach):
    return (
        extended(value_rows, (("row", 0), ("col", 1)), window_reach),
        extended(valid_mask, (("row", 0), ("col", 1)), window_reach),
    )


def gather_stats(stats):
    return joined((stats[0], stats[1], stats[2]), ("row", "col"), combine_stats)


def shards(tokens, registers, tile_mask, w_qkv, w_out, w_up, w_down, norm_attn, norm_mlp):
    grid_rows, grid_columns, window_width = tokens.shape
    valid_mask = jnp.repeat(jnp.repeat(tile_mask, 8, axis=0), 8, axis=1).astype(jnp.bfloat16)
    x, g = (tokens, registers)
    for attention_layer in range(LAYERS):
        dilation_step = dilation_list[attention_layer % 2]
        window_reach = 6 * dilation_step
        weights = w_qkv[attention_layer]
        h = layer_norm(x, norm_attn[attention_layer]).astype(jnp.bfloat16)
        hg = layer_norm(g, norm_attn[attention_layer]).astype(jnp.bfloat16)
        rqkv = jnp.dot(hg, weights, preferred_element_type=jnp.float32).astype(jnp.bfloat16)
        reg_q, register_keys, register_values = (
            rqkv[:, :window_width],
            rqkv[:, window_width : 2 * window_width],
            rqkv[:, 2 * window_width :],
        )
        qkv = jnp.dot(h, weights, preferred_element_type=jnp.float32).astype(jnp.bfloat16)
        query_rows = qkv[..., :window_width]
        pairs = qkv[..., window_width:]
        pairs_pad, mask_padded = extend_rim(pairs, valid_mask, window_reach)
        k_local, v_local = (pairs[..., :window_width], pairs[..., window_width:])
        key_padded, value_padded = (pairs_pad[..., :window_width], pairs_pad[..., window_width:])
        stats = register_partial(
            reg_q,
            k_local.reshape(-1, window_width),
            v_local.reshape(-1, window_width),
            valid_mask.reshape(-1),
        )
        attended_output = gather_neighbour_block(
            query_rows,
            key_padded,
            value_padded,
            mask_padded,
            register_keys,
            register_values,
            dilation_step,
        )
        merged = gather_stats(stats)
        reg_att = finish_registers(merged, reg_q, register_keys, register_values)
        x = (
            x.astype(jnp.float32)
            + jnp.dot(attended_output, w_out[attention_layer], preferred_element_type=jnp.float32)
        ).astype(jnp.bfloat16)
        g = (
            g.astype(jnp.float32)
            + jnp.dot(reg_att, w_out[attention_layer], preferred_element_type=jnp.float32)
        ).astype(jnp.bfloat16)
        h2 = layer_norm(x, norm_mlp[attention_layer]).astype(jnp.bfloat16)
        hg2 = layer_norm(g, norm_mlp[attention_layer]).astype(jnp.bfloat16)
        inner = jax.nn.gelu(
            jnp.dot(h2, w_up[attention_layer], preferred_element_type=jnp.float32)
        ).astype(jnp.bfloat16)
        inner_g = jax.nn.gelu(
            jnp.dot(hg2, w_up[attention_layer], preferred_element_type=jnp.float32)
        ).astype(jnp.bfloat16)
        x = (
            x.astype(jnp.float32)
            + jnp.dot(inner, w_down[attention_layer], preferred_element_type=jnp.float32)
        ).astype(jnp.bfloat16)
        g = (
            g.astype(jnp.float32)
            + jnp.dot(inner_g, w_down[attention_layer], preferred_element_type=jnp.float32)
        ).astype(jnp.bfloat16)
    return (x, g)


def solution(mesh):
    return jax.shard_map(
        shards,
        mesh=mesh,
        in_specs=(P("row", "col", None), P(), P("row", "col"), P(), P(), P(), P(), P(), P()),
        out_specs=(P("row", "col", None), P()),
        check_vma=False,
    )
```

profile of v0, /device:TPU:1, one launch (start us, length us, event | category | flops | bytes accessed | tf_op | source)
XLA Modules:
  0.0 817.9 jit_solution(109063029461515327)
XLA Ops:
  43.2 4.7 collective-permute-start
  57.8 4.6 collective-permute-start.12
  68.8 41.4 %all-gather.5 = f32[32,64,8]{1,2,0:T(8,128)S(1)} all-gather(f32[1,64,8]{1,2,0:T(8,128)S(1)} %bitcast.796), channel_id=3, replica_groups=mesh['row'=4,'col'=8] {'row','col'}, dimensions={0}, use_global_device_ids=true | all-gather | bytes 67584 | tf_op jit(solution)/shard_map/all_gather | solution.py:31
  111.5 37.0 %all-gather.4 = f32[32,64,8]{1,2,0:T(8,128)S(1)} all-gather(f32[1,64,8]{1,2,0:T(8,128)S(1)} %bitcast.795), channel_id=2, replica_groups=mesh['row'=4,'col'=8] {'row','col'}, dimensions={0}, use_global_device_ids=true | all-gather | bytes 67584 | tf_op jit(solution)/shard_map/all_gather | solution.py:31
  189.0 7.5 collective-permute-done.3
  202.4 4.8 copy.311
  209.0 4.8 copy.289
  214.9 144.9 %while.62 = (s32[]{:T(128)}, bf16[9,4,64,256]{3,2,1,0:T(8,128)(2,1)}, bf16[9,4,576,256]{3,2,1,0:T(8,128)(2,1)}, bf16[9,4,576]{2,1,0:T(4,128)(2,1)}, bf16[9,4,64,...) while((s32[]{:T(128)}, ...), condition=%wide.region_9.10_spmd.clone, body=%wide.region_4.9_spmd.clone.sunk | while | flops 182003968 | bytes 49372368 | solution.py:184
  363.9 5.2 convert_reduce_fusion.1
  377.6 4.9 collective-permute-done.8
  388.3 8.4 %collective-permute-start.10 = (bf16[72,12,512]{2,0,1:T(8,128)(2,1)}, bf16[72,12,512]{2,0,1:T(8,128)(2,1)}, u32[]{:S(2)}, u32[]{:S(2)}) collective-permute-start(bf16[72,12,512]{2,0,1:T(8,128)(2,1)} %copy.319), channel_id=1, source_target_pairs={{0,1},{1,2},{2,3},{3,4},{4,5},{5,6},{6,7},{8,9},{9,10},{10,11},{11... | collective-permute-start | bytes 2654216 | tf_op jit(solution)/shard_map/ppermute | solution.py:22
  405.8 5.3 copy.351
  411.1 5.5 reshape_reshape.54
  416.6 5.1 copy.353
  421.7 5.5 reshape_reshape.55
  434.0 9.8 %pad_maximum_fusion = bf16[72,72,512]{2,1,0:T(8,128)(2,1)S(1)} fusion(bf16[72,12,512]{2,1,0:T(8,128)(2,1)S(1)} %copy.322, bf16[12,48,512]{2,1,0:T(8,128)(2,1)S(1)} %copy-done.17, bf16[48,48,512]{2,1,0:T(8,128)(2,1)S(1)} %slice.488, bf16[12,48,512]{2,1,0:T(8,128)(2,1)S(1)} %copy-done.15, bf16[72,12,512]{2,1,0:T(8,128)(2,1)S(1)} %copy.321), kind=kLoop, calls=%fused_computation.102 | loop fusion | flops 26542080 | bytes 10616832 | tf_op jit(solution)/shard_map/concatenate | solution.py:26
  452.5 4.9 copy.334
  464.2 4.8 copy.325
  470.2 53.6 %while.60 = (s32[]{:T(128)}, f32[64,8]{0,1:T(8,128)S(1)}, f32[64,8]{0,1:T(8,128)S(1)}, f32[64,256]{0,1:T(8,128)S(1)}, f32[32,64,8]{1,2,0:T(8,128)}, /*index=5*/f...) while((s32[]{:T(128)}, f32[64,8]{0,1:T(8,128)S(1)}, ...), condition=%wide.region_17.18_spmd, body=%wide.region_16.17_spmd.sunk | while | flops 52229 | bytes 479383 | solution.py:36
  533.1 150.7 %while.63 = (s32[]{:T(128)}, bf16[9,4,64,256]{3,2,1,0:T(8,128)(2,1)}, bf16[9,4,576,256]{3,2,1,0:T(8,128)(2,1)}, bf16[9,4,576]{2,1,0:T(4,128)(2,1)}, bf16[9,4,64,...) while((s32[]{:T(128)}, ...), condition=%wide.region_29.30_spmd.clone, body=%wide.region_24.29_spmd.clone.sunk | while | flops 182003968 | bytes 49373428 | solution.py:184
  690.8 38.6 %all-gather.7 = f32[32,64,8]{1,2,0:T(8,128)S(1)} all-gather(f32[1,64,8]{1,2,0:T(8,128)S(1)} %bitcast.797), channel_id=5, replica_groups=mesh['row'=4,'col'=8] {'row','col'}, dimensions={0}, use_global_device_ids=true | all-gather | bytes 67584 | tf_op jit(solution)/shard_map/all_gather | solution.py:31
  729.4 37.2 %all-gather.6 = f32[32,64,8]{1,2,0:T(8,128)S(1)} all-gather(f32[1,64,8]{1,2,0:T(8,128)S(1)} %bitcast.794), channel_id=4, replica_groups=mesh['row'=4,'col'=8] {'row','col'}, dimensions={0}, use_global_device_ids=true | all-gather | bytes 67584 | tf_op jit(solution)/shard_map/all_gather | solution.py:31
  768.3 6.0 fusion.105
  775.4 32.4 %while.61 = (s32[]{:T(128)}, f32[64,8]{0,1:T(8,128)S(1)}, f32[64,8]{0,1:T(8,128)S(1)}, f32[64,256]{0,1:T(8,128)S(1)}, f32[32,64,8]{1,2,0:T(8,128)S(1)}, /*index=...) while((s32[]{:T(128)}, f32[64,8]{0,1:T(8,128)S(1)}, ...), condition=%wide.region_35.36_spmd, body=%wide.region_34.35_spmd.sunk | while | flops 52229 | bytes 479383 | solution.py:36
  (1026 shorter events, 550.9 us)
Async XLA Ops:
  7.2 462.0 %all-gather.11.cloned.1.call-start = ((), (), s32[]{:S(2)}) async-start(), calls=%async_computation | async-start | bytes 2162688 | tf_op jit(solution)/shard_map/all_gather | solution.py:31
  41.2 733.1 %all-gather.13.cloned.1.call-start = ((), (), s32[]{:S(2)}) async-start(), calls=%async_computation.1 | async-start | bytes 2162688 | tf_op jit(solution)/shard_map/all_gather | solution.py:31
  43.2 135.4 %collective-permute-start = (bf16[6,48,512]{2,1,0:T(8,128)(2,1)}, bf16[6,48,512]{2,1,0:T(8,128)(2,1)}, u32[]{:S(2)}, u32[]{:S(2)}) collective-permute-start(bf16[6,48,512]{2,1,0:T(8,128)(2,1)} %get-tuple-element.830), channel_id=1, source_target_pairs={{0,8},{8,16},{16,24},{1,9},{9,17},{17,25},{2,10},{10,18},{18,26},{... | collective-permute-start | bytes 884744 | tf_op jit(solution)/shard_map/ppermute | solution.py:22
  47.9 130.7 %collective-permute-start.1 = (bf16[6,48,512]{2,1,0:T(8,128)(2,1)}, bf16[6,48,512]{2,1,0:T(8,128)(2,1)}, u32[]{:S(2)}, u32[]{:S(2)}) collective-permute-start(bf16[6,48,512]{2,1,0:T(8,128)(2,1)} %get-tuple-element.831), channel_id=1, source_target_pairs={{8,0},{16,8},{24,16},{9,1},{17,9},{25,17},{10,2},{18,10},{26,18},{... | collective-permute-start | bytes 884744 | tf_op jit(solution)/shard_map/ppermute | solution.py:25
  50.2 108.2 %collective-permute-start.4 = (bf16[6,48]{0,1:T(8,128)(2,1)}, bf16[6,48]{0,1:T(8,128)(2,1)}, u32[]{:S(2)}, u32[]{:S(2)}) collective-permute-start(bf16[6,48]{0,1:T(8,128)(2,1)} %broadcast_bitcast_fusion.5), channel_id=1, source_target_pairs={{0,8},{8,16},{16,24},{1,9},{9,17},{17,25},{2,10},{10,18},{18,26},{... | collective-permute-start | bytes 1736 | tf_op jit(solution)/shard_map/ppermute | solution.py:22
  55.4 104.4 %collective-permute-start.5 = (bf16[6,48]{0,1:T(8,128)(2,1)}, bf16[6,48]{0,1:T(8,128)(2,1)}, u32[]{:S(2)}, u32[]{:S(2)}) collective-permute-start(bf16[6,48]{0,1:T(8,128)(2,1)} %broadcast_bitcast_fusion.3), channel_id=1, source_target_pairs={{8,0},{16,8},{24,16},{9,1},{17,9},{25,17},{10,2},{18,10},{26,18},{... | collective-permute-start | bytes 1736 | tf_op jit(solution)/shard_map/ppermute | solution.py:25
  57.8 106.1 %collective-permute-start.12 = (bf16[12,48]{0,1:T(8,128)(2,1)}, bf16[12,48]{0,1:T(8,128)(2,1)}, u32[]{:S(2)}, u32[]{:S(2)}) collective-permute-start(bf16[12,48]{0,1:T(8,128)(2,1)} %broadcast_bitcast_fusion.2), channel_id=1, source_target_pairs={{0,8},{8,16},{16,24},{1,9},{9,17},{17,25},{2,10},{10,18},{18,26},{... | collective-permute-start | bytes 3464 | tf_op jit(solution)/shard_map/ppermute | solution.py:22
  65.7 91.4 %copy-start.9 = (bf16[48,48,256]{2,1,0:T(8,128)(2,1)S(1)}, bf16[48,48,256]{2,1,0:T(8,128)(2,1)}, u32[]{:S(2)}) copy-start(bf16[48,48,256]{2,1,0:T(8,128)(2,1)} %get-tuple-element.825) | copy-start | bytes 3538948
  158.4 7.5 collective-permute-start.13
  160.6 9.7 %collective-permute-start.6 = (bf16[60,6]{0,1:T(8,128)(2,1)S(1)}, bf16[60,6]{0,1:T(8,128)(2,1)S(1)}, u32[]{:S(2)}, u32[]{:S(2)}) collective-permute-start(bf16[60,6]{0,1:T(8,128)(2,1)S(1)} %get-tuple-element.842), channel_id=1, source_target_pairs={{0,1},{1,2},{2,3},{3,4},{4,5},{5,6},{6,7},{8,9},{9,10},{10,11},{11... | collective-permute-start | bytes 2168 | tf_op jit(solution)/shard_map/ppermute | solution.py:22
  163.9 8.5 %collective-permute-start.7 = (bf16[60,6]{0,1:T(8,128)(2,1)S(1)}, bf16[60,6]{0,1:T(8,128)(2,1)S(1)}, u32[]{:S(2)}, u32[]{:S(2)}) collective-permute-start(bf16[60,6]{0,1:T(8,128)(2,1)S(1)} %get-tuple-element.843), channel_id=1, source_target_pairs={{1,0},{2,1},{3,2},{4,3},{5,4},{6,5},{7,6},{9,8},{10,9},{11,10},{12... | collective-permute-start | bytes 2168 | tf_op jit(solution)/shard_map/ppermute | solution.py:25
  166.7 9.0 %collective-permute-start.14 = (bf16[72,12]{0,1:T(8,128)(2,1)S(1)}, bf16[72,12]{0,1:T(8,128)(2,1)S(1)}, u32[]{:S(2)}, u32[]{:S(2)}) collective-permute-start(bf16[72,12]{0,1:T(8,128)(2,1)S(1)} %get-tuple-element.840), channel_id=1, source_target_pairs={{0,1},{1,2},{2,3},{3,4},{4,5},{5,6},{6,7},{8,9},{9,10},{10,11},{11... | collective-permute-start | bytes 5192 | tf_op jit(solution)/shard_map/ppermute | solution.py:22
  170.3 5.3 collective-permute-start.15
  179.6 9.4 %collective-permute-start.2 = (bf16[60,6,512]{2,1,0:T(8,128)(2,1)S(1)}, bf16[60,6,512]{2,1,0:T(8,128)(2,1)S(1)}, u32[]{:S(2)}, u32[]{:S(2)}) collective-permute-start(bf16[60,6,512]{2,1,0:T(8,128)(2,1)S(1)} %get-tuple-element.832), channel_id=1, source_target_pairs={{0,1},{1,2},{2,3},{3,4},{4,5},{5,6},{6,7},{8,9},{9,10},{10,11},{11... | collective-permute-start | bytes 1105928 | tf_op jit(solution)/shard_map/ppermute | solution.py:22
  183.3 13.2 %collective-permute-start.3 = (bf16[60,6,512]{2,1,0:T(8,128)(2,1)S(1)}, bf16[60,6,512]{2,1,0:T(8,128)(2,1)S(1)}, u32[]{:S(2)}, u32[]{:S(2)}) collective-permute-start(bf16[60,6,512]{2,1,0:T(8,128)(2,1)S(1)} %get-tuple-element.833), channel_id=1, source_target_pairs={{1,0},{2,1},{3,2},{4,3},{5,4},{6,5},{7,6},{9,8},{10,9},{11,10},{12... | collective-permute-start | bytes 1105928 | tf_op jit(solution)/shard_map/ppermute | solution.py:25
  371.8 10.8 %collective-permute-start.8 = (bf16[12,48,512]{2,1,0:T(8,128)(2,1)S(1)}, bf16[12,48,512]{2,1,0:T(8,128)(2,1)S(1)}, u32[]{:S(2)}, u32[]{:S(2)}) collective-permute-start(bf16[12,48,512]{2,1,0:T(8,128)(2,1)S(1)} %get-tuple-element.828), channel_id=1, source_target_pairs={{0,8},{8,16},{16,24},{1,9},{9,17},{17,25},{2,10},{10,18},{18,26},{... | collective-permute-start | bytes 1769480 | tf_op jit(solution)/shard_map/ppermute | solution.py:22
  375.8 10.6 %collective-permute-start.9 = (bf16[12,48,512]{2,1,0:T(8,128)(2,1)S(1)}, bf16[12,48,512]{2,1,0:T(8,128)(2,1)S(1)}, u32[]{:S(2)}, u32[]{:S(2)}) collective-permute-start(bf16[12,48,512]{2,1,0:T(8,128)(2,1)S(1)} %get-tuple-element.829), channel_id=1, source_target_pairs={{8,0},{16,8},{24,16},{9,1},{17,9},{25,17},{10,2},{18,10},{26,18},{... | collective-permute-start | bytes 1769480 | tf_op jit(solution)/shard_map/ppermute | solution.py:25
  388.3 42.7 %collective-permute-start.10 = (bf16[72,12,512]{2,0,1:T(8,128)(2,1)}, bf16[72,12,512]{2,0,1:T(8,128)(2,1)}, u32[]{:S(2)}, u32[]{:S(2)}) collective-permute-start(bf16[72,12,512]{2,0,1:T(8,128)(2,1)} %copy.319), channel_id=1, source_target_pairs={{0,1},{1,2},{2,3},{3,4},{4,5},{5,6},{6,7},{8,9},{9,10},{10,11},{11... | collective-permute-start | bytes 2654216 | tf_op jit(solution)/shard_map/ppermute | solution.py:22
  398.2 34.3 %collective-permute-start.11 = (bf16[72,12,512]{2,0,1:T(8,128)(2,1)}, bf16[72,12,512]{2,0,1:T(8,128)(2,1)}, u32[]{:S(2)}, u32[]{:S(2)}) collective-permute-start(bf16[72,12,512]{2,0,1:T(8,128)(2,1)} %copy.320), channel_id=1, source_target_pairs={{1,0},{2,1},{3,2},{4,3},{5,4},{6,5},{7,6},{9,8},{10,9},{11,10},{12... | collective-permute-start | bytes 2654216 | tf_op jit(solution)/shard_map/ppermute | solution.py:25
  470.2 57.1 %copy-start.10 = (bf16[2304,8,32]{0,2,1:T(8,128)(2,1)S(1)}, bf16[2304,8,32]{0,2,1:T(8,128)(2,1)}, u32[]{:S(2)}) copy-start(bf16[2304,8,32]{0,2,1:T(8,128)(2,1)} %reshape_reshape.54) | copy-start | bytes 3538948
  686.9 79.7 %copy-start.26 = (bf16[64,256]{0,1:T(8,128)(2,1)S(1)}, bf16[64,256]{0,1:T(8,128)(2,1)}, u32[]{:S(2)}) copy-start(bf16[64,256]{0,1:T(8,128)(2,1)} %copy-done.25) | copy-start | bytes 98308
  687.4 79.5 %copy-start.8 = (bf16[48,48,256]{2,1,0:T(8,128)(2,1)S(1)}, bf16[48,48,256]{2,1,0:T(8,128)(2,1)}, u32[]{:S(2)}) copy-start(bf16[48,48,256]{2,1,0:T(8,128)(2,1)} %copy-done.7) | copy-start | bytes 3538948
  687.4 79.5 %copy-start.22 = (bf16[2,256,256]{2,1,0:T(8,128)(2,1)S(1)}, bf16[2,256,256]{2,1,0:T(8,128)(2,1)}, u32[]{:S(2)}) copy-start(bf16[2,256,256]{2,1,0:T(8,128)(2,1)} %param.21) | copy-start | bytes 786436
  690.8 77.5 %copy-start.60 = (f32[1,256]{1,0:T(1,128)S(1)}, f32[1,256]{1,0:T(1,128)}, u32[]{:S(2)}) copy-start(f32[1,256]{1,0:T(1,128)} %get-tuple-element.844) | copy-start | bytes 3076
  (98 other events, 1064.2 us)
Sparse Core Ops, SparseCore 0:
  41.4 59.0 all-gather.10
  531.3 53.8 all-gather.12
where the time goes:
time: 834 us; the launch traced here: 818 us
  local copies, waits for them, and re-layouts  328 us (39%)
  blocking collectives  154 us (18%)
  matrix products  133 us (16%)
  other arithmetic  112 us (13%)
  starting transfers between devices  50.1 us (6%)
  waiting for transfers between devices  18.8 us (2%)
  between operations  16.2 us (2%)
    all_gather x4, blocking collectives, joined(): gathered = jax.tree.map(lambda a: lax.all_gather(a, axis), part)  154 us
    dynamic_slice x90, local copies, waits for them, and re-layouts, gather_neighbour_block(): lax.map(one, (query_tiles.reshape((count // group, group) + query_tiles.s...  114 us
    dot_general x18, matrix products, tile_attention(): jnp.einsum('thqk,tkhe->tqhe', near_w.astype(jnp.bfloat16), v4, preferred_...  70.2 us
    dynamic_slice x128, local copies, waits for them, and re-layouts, take(): lax.dynamic_index_in_dim(a, source, 0, False)  59.6 us
    ppermute x8, starting transfers between devices, extended(): lax.ppermute(lax.slice_in_dim(block, block.shape[dim] - width, None, axis...  36.9 us
    reduce_sum x36, other arithmetic, tile_attention(): total = jnp.sum(near_w, axis=-1) + jnp.sum(far_w, axis=-1)  31.7 us
    slice x6, local copies, waits for them, and re-layouts, shards(): k_local, v_local = (pairs[..., :window_width], pairs[..., window_width:])  23.9 us
    add x62, other arithmetic, combine_stats(): first[1] * fa + second[1] * fb  22.3 us
  transfers between devices with their start and end apart: 18, of which 4 were waited for; matrix products, arithmetic and copies ran while one was open for 53% of the time, Pallas kernels for 0%

commit v1 on v0

v1 whole, which is shorter than its diff:
```python
import functools
import math

import jax
import jax.numpy as jnp
from jax import lax
from jax.experimental import pallas as pl
from jax.experimental.pallas import tpu as pltpu
from jax.sharding import PartitionSpec as P

HEADS = 8
HEAD = 32
WIDTH = 256
REGS = 64
TILE = 8
LAYERS = 2
DILATIONS = (1, 2)
REACH = 6
QROWS = 4
KROWS = QROWS + 2 * REACH
KEYS = 3 * KROWS * TILE
QTILE = QROWS * TILE
CHUNK = 256
NEG = -1e30
EPS = 1e-05
SCALE = math.log2(math.e) * HEAD**-0.5
F32 = jnp.float32
BF16 = jnp.bfloat16
VMEM_LIMIT = 60 * 1024 * 1024


def mm(a, b):
    return lax.dot_general(a, b, (((1,), (0,)), ((), ())), preferred_element_type=F32)


def mm_nt(a, b):
    return lax.dot_general(a, b, (((1,), (1,)), ((), ())), preferred_element_type=F32)


def normed(x, gain):
    v = x.astype(F32)
    mean = jnp.mean(v, axis=-1, keepdims=True)
    centred = v - mean
    spread = jnp.mean(centred * centred, axis=-1, keepdims=True)
    return (centred * lax.rsqrt(spread + EPS) * gain).astype(BF16)


def iota(shape, dim):
    return lax.broadcasted_iota(jnp.int32, shape, dim)


def ones_where(cond):
    return jnp.where(cond, 1.0, 0.0).astype(BF16)


def head_mask(rows_per_head):
    shape = (HEADS * rows_per_head, WIDTH)
    return ones_where(iota(shape, 0) // rows_per_head == iota(shape, 1) // HEAD)


def spread_heads(q, mask):
    return jnp.concatenate([q] * HEADS, axis=0) * mask


def diagonal(part):
    lane = iota((HEAD, WIDTH), 1) // REGS
    out = jnp.zeros((HEAD, WIDTH), F32)
    for b in range(WIDTH // REGS):
        out = out + jnp.where(lane == b, part[b * HEAD : (b + 1) * HEAD, :], 0.0)
    return out


def mlp(x, h2, w_up, w_down):
    u = jax.nn.gelu(mm(h2, w_up), approximate=True).astype(BF16)
    return (x.astype(F32) + mm(u, w_down)).astype(BF16)


def stats_kernel(x_ref, g_ref, bias_ref, wq_ref, wk_ref, wvt_ref, gain_ref, out_ref, t_ref, vt_ref):
    chunks = x_ref.shape[0] // CHUNK
    gain = gain_ref[...]
    rq = mm(normed(g_ref[...], gain), wq_ref[...]).astype(BF16)
    rq_bd = spread_heads(rq, head_mask(REGS))

    def first(i, top):
        rows = pl.ds(pl.multiple_of(i * CHUNK, CHUNK), CHUNK)
        h = normed(x_ref[rows, :], gain)
        k = mm(h, wk_ref[...]).astype(BF16)
        vt_ref[i] = mm_nt(wvt_ref[...], h).astype(BF16)
        bias = bias_ref[rows, :].astype(F32)
        t = mm_nt(k, rq_bd) * SCALE + jnp.concatenate([bias] * 4, axis=1)
        t_ref[rows, :] = t
        return jnp.maximum(top, jnp.max(t, axis=0, keepdims=True))

    top = lax.fori_loop(0, chunks, first, jnp.full((1, 2 * WIDTH), 3 * NEG, F32))

    def second(i, carry):
        total, n0, n1 = carry
        rows = pl.ds(pl.multiple_of(i * CHUNK, CHUNK), CHUNK)
        w = jnp.exp2(t_ref[rows, :] - top)
        total = total + jnp.sum(w, axis=0, keepdims=True)
        wb = w.astype(BF16)
        vt = vt_ref[i]
        n0 = n0 + mm(vt[:128], wb[:, :WIDTH])
        n1 = n1 + mm(vt[128:], wb[:, WIDTH:])
        return total, n0, n1

    zero = jnp.zeros((128, WIDTH), F32)
    total, n0, n1 = lax.fori_loop(
        0, chunks, second, (jnp.zeros((1, 2 * WIDTH), F32), zero, zero)
    )
    out_ref[0:HEAD, :] = jnp.concatenate([diagonal(n0), diagonal(n1)], axis=1)
    rest = iota((8, 2 * WIDTH), 0)
    out_ref[HEAD : HEAD + 8, :] = jnp.where(rest == 0, top, jnp.where(rest == 1, total, 0.0))


def finish_kernel(
    stats_ref, g_ref, wq_ref, wk_ref, wvt_ref, gain_ref, wo_ref, wu_ref, wd_ref, gain2_ref, out_ref
):
    g = g_ref[...]
    hg = normed(g, gain_ref[...])
    rq = mm(hg, wq_ref[...]).astype(BF16)
    rk = mm(hg, wk_ref[...]).astype(BF16)
    rvt = mm_nt(wvt_ref[...], hg).astype(BF16)
    rq_bd = spread_heads(rq, head_mask(REGS))
    own = mm_nt(rk, rq_bd) * SCALE
    own_top = jnp.max(own, axis=0, keepdims=True)
    w = jnp.exp2(own - own_top)
    own_total = jnp.sum(w, axis=0, keepdims=True)
    wb = w.astype(BF16)
    own_numer = jnp.concatenate(
        [diagonal(mm(rvt[:128], wb[:, :WIDTH])), diagonal(mm(rvt[128:], wb[:, WIDTH:]))], axis=1
    )
    top = stats_ref[HEAD : HEAD + 1, :]
    total = stats_ref[HEAD + 1 : HEAD + 2, :]
    peak = jnp.maximum(top, own_top)
    keep = jnp.exp2(top - peak)
    keep_own = jnp.exp2(own_top - peak)
    total = total * keep + own_total * keep_own
    z = ((stats_ref[0:HEAD, :] * keep + own_numer * keep_own) / total).astype(BF16)
    shape = (WIDTH, HEADS * REGS)
    mask = ones_where(iota(shape, 0) // HEAD == iota(shape, 1) // REGS)
    z = jnp.concatenate([z] * HEADS, axis=0) * mask
    pick_shape = (REGS, HEADS * REGS)
    pick = ones_where(iota(pick_shape, 0) == iota(pick_shape, 1) % REGS)
    attended = mm_nt(pick, z).astype(BF16)
    g = (g.astype(F32) + mm(attended, wo_ref[...])).astype(BF16)
    out_ref[...] = mlp(g, normed(g, gain2_ref[...]), wu_ref[...], wd_ref[...])


def layer_kernel(
    x_ref, bias_ref, g_ref, wq_ref, wk_ref, wvt_ref, gain_ref, wo_ref, wu_ref, wd_ref, gain2_ref,
    out_ref, h_ref, k_ref, q_ref, vt_ref, win_ref, mask_ref, att_ref,
):
    grids, groups, key_rows, _ = x_ref.shape
    own_groups, rows = groups - 2, key_rows - 2 * REACH * TILE
    strips = rows // QTILE
    own = pl.ds(REACH * TILE, rows)
    gain = gain_ref[...]

    hg = normed(g_ref[...], gain)
    rk = mm(hg, wk_ref[...]).astype(BF16)
    rvt = mm_nt(wvt_ref[...], hg).astype(BF16)
    mask_ref[...] = head_mask(QTILE)
    shape = (KEYS, 128)
    key, query = iota(shape, 0), iota(shape, 1) % QTILE
    row_step = (key % (KROWS * TILE)) // TILE - query // TILE
    col_step = (key // (KROWS * TILE) - 1) * TILE + key % TILE - query % TILE
    near = (row_step >= 0) & (row_step <= 2 * REACH) & (col_step >= -REACH) & (col_step <= REACH)
    win_ref[...] = jnp.where(near, 0.0, NEG)

    def project(n, carry):
        gr, c = n // groups, n % groups
        h = normed(x_ref[gr, c], gain)
        h_ref[gr, c] = h
        k_ref[gr, c] = mm(h, wk_ref[...]).astype(BF16)
        return carry

    lax.fori_loop(0, grids * groups, project, 0)

    def queries(n, carry):
        gr, c = n // own_groups, n % own_groups
        q_ref[gr, c] = mm(h_ref[gr, c + 1, own, :], wq_ref[...]).astype(BF16)
        return carry

    lax.fori_loop(0, grids * own_groups, queries, 0)

    half = (128, 128)
    diag = iota(half, 0) // HEAD == iota(half, 1) // QTILE
    pick_shape = (QTILE, 128)
    pick = ones_where(iota(pick_shape, 0) == iota(pick_shape, 1) % QTILE)

    def strip(n, carry):
        gr, i = n // strips, n % strips
        start = pl.multiple_of(i * QTILE, QTILE)
        key_at = pl.ds(start, KROWS * TILE)
        hs = h_ref[gr, :, key_at, :].reshape(groups * KROWS * TILE, WIDTH)
        vt_ref[...] = mm_nt(wvt_ref[...], hs).astype(BF16)
        for j in range(own_groups):
            q = q_ref[gr, j, pl.ds(start, QTILE), :]
            q_bd = spread_heads(q, mask_ref[...])
            k = k_ref[gr, j : j + 3, key_at, :].reshape(KEYS, WIDTH)
            bias = bias_ref[gr, j : j + 3, key_at, :].reshape(KEYS, 128).astype(F32) + win_ref[...]
            s = mm_nt(jnp.concatenate([k, rk], axis=0), q_bd) * SCALE
            near_s = s[:KEYS] + jnp.concatenate([bias, bias], axis=1)
            far_s = s[KEYS:]
            top = jnp.maximum(
                jnp.max(near_s, axis=0, keepdims=True), jnp.max(far_s, axis=0, keepdims=True)
            )
            near_w = jnp.exp2(near_s - top)
            far_w = jnp.exp2(far_s - top)
            total = jnp.sum(near_w, axis=0, keepdims=True) + jnp.sum(far_w, axis=0, keepdims=True)
            w = jnp.concatenate([near_w.astype(BF16), far_w.astype(BF16)], axis=0)
            inverse = 1.0 / total
            lanes = slice(j * KROWS * TILE, j * KROWS * TILE + KEYS)
            parts = []
            for a in range(2):
                part = slice(128 * a, 128 * a + 128)
                vt = jnp.concatenate([vt_ref[part, lanes], rvt[part]], axis=1)
                o = mm(vt, w[:, part]) * inverse[:, part]
                parts.append(mm_nt(pick, jnp.where(diag, o, 0.0).astype(BF16)))
            att_ref[gr, j, pl.ds(start, QTILE), :] = jnp.concatenate(parts, axis=1).astype(BF16)
        return carry

    lax.fori_loop(0, grids * strips, strip, 0)

    def tail(n, carry):
        gr, c = n // own_groups, n % own_groups
        x = x_ref[gr, c + 1, own, :]
        x = (x.astype(F32) + mm(att_ref[gr, c], wo_ref[...])).astype(BF16)
        out_ref[gr, c] = mlp(x, normed(x, gain2_ref[...]), wu_ref[...], wd_ref[...])
        return carry

    lax.fori_loop(0, grids * own_groups, tail, 0)


def params():
    return pltpu.CompilerParams(vmem_limit_bytes=VMEM_LIMIT)


def register_stats(x, g, bias, w):
    tokens = x.shape[0]
    return pl.pallas_call(
        stats_kernel,
        out_shape=jax.ShapeDtypeStruct((HEAD + 8, HEADS * REGS), F32),
        scratch_shapes=[
            pltpu.VMEM((tokens, HEADS * REGS), F32),
            pltpu.VMEM((tokens // CHUNK, WIDTH, CHUNK), BF16),
        ],
        compiler_params=params(),
        name="register_stats",
    )(x, g, bias, w["q"], w["k"], w["vt"], w["gain"])


def finish_registers(stats, g, w):
    return pl.pallas_call(
        finish_kernel,
        out_shape=jax.ShapeDtypeStruct(g.shape, BF16),
        compiler_params=params(),
        name="finish_registers",
    )(
        stats, g, w["q"], w["k"], w["vt"], w["gain"], w["out"], w["up"], w["down"], w["gain2"]
    )


def token_layer(x, bias, g, w):
    grids, groups, key_rows, _ = x.shape
    own = (grids, groups - 2, key_rows - 2 * REACH * TILE, WIDTH)
    return pl.pallas_call(
        layer_kernel,
        out_shape=jax.ShapeDtypeStruct(own, BF16),
        scratch_shapes=[
            pltpu.VMEM(x.shape, BF16),
            pltpu.VMEM(x.shape, BF16),
            pltpu.VMEM(own, BF16),
            pltpu.VMEM((WIDTH, groups * KROWS * TILE), BF16),
            pltpu.VMEM((KEYS, 128), F32),
            pltpu.VMEM((HEADS * QTILE, WIDTH), BF16),
            pltpu.VMEM(own, BF16),
        ],
        compiler_params=params(),
        name="token_layer",
    )(
        x, bias, g, w["q"], w["k"], w["vt"], w["gain"], w["out"], w["up"], w["down"], w["gain2"]
    )


def combine(a, b):
    top_a, top_b = a[HEAD : HEAD + 1], b[HEAD : HEAD + 1]
    peak = jnp.maximum(top_a, top_b)
    fa, fb = jnp.exp2(top_a - peak), jnp.exp2(top_b - peak)
    out = a * fa + b * fb
    row = lax.broadcasted_iota(jnp.int32, out.shape, 0)
    return jnp.where(row == HEAD, peak, out)


def joined(stats):
    for axis in ("col", "row"):
        count = lax.axis_size(axis)
        step = 1
        while step < count:
            other = lax.ppermute(stats, axis, [(i, i ^ step) for i in range(count)])
            stats = combine(stats, other)
            step *= 2
    return stats


def extended(block, widths):
    for (axis, dim), width in zip((("row", 0), ("col", 1)), widths):
        count = lax.axis_size(axis)
        forward = [(i, i + 1) for i in range(count - 1)]
        backward = [(target, source) for source, target in forward]
        size = block.shape[dim]
        low = lax.ppermute(
            lax.slice_in_dim(block, size - width, size, axis=dim), axis, forward
        )
        high = lax.ppermute(lax.slice_in_dim(block, 0, width, axis=dim), axis, backward)
        block = jnp.concatenate([low, block, high], axis=dim)
    return block


def to_groups(x, dil):
    rows, cols = x.shape[:2]
    rest = x.shape[2:]
    x = x.reshape((rows // dil, dil, cols // (dil * TILE), TILE, dil) + rest)
    x = jnp.transpose(x, (1, 4, 2, 0, 3) + tuple(range(5, x.ndim)))
    return x.reshape((dil * dil, cols // (dil * TILE), rows // dil * TILE) + rest)


def from_groups(x, dil, rows, cols):
    x = x.reshape(dil, dil, cols // (dil * TILE), rows // dil, TILE, WIDTH)
    return jnp.transpose(x, (3, 0, 2, 4, 1, 5)).reshape(rows, cols, WIDTH)


def layer_weights(l, w_qkv, w_out, w_up, w_down, norm_attn, norm_mlp):
    return {
        "q": w_qkv[l, :, :WIDTH],
        "k": w_qkv[l, :, WIDTH : 2 * WIDTH],
        "vt": w_qkv[l, :, 2 * WIDTH :].T,
        "out": w_out[l],
        "up": w_up[l],
        "down": w_down[l],
        "gain": norm_attn[l : l + 1],
        "gain2": norm_mlp[l : l + 1],
    }


def shards(tokens, registers, tile_mask, w_qkv, w_out, w_up, w_down, norm_attn, norm_mlp):
    rows, cols, _ = tokens.shape
    tiles = extended(tile_mask.astype(BF16), (2, 2))
    x, g = tokens, registers
    for l in range(LAYERS):
        dil = DILATIONS[l % 2]
        w = layer_weights(l, w_qkv, w_out, w_up, w_down, norm_attn, norm_mlp)
        row_halo, col_halo = REACH * dil, TILE * dil
        valid = jnp.repeat(jnp.repeat(tiles, TILE, axis=0), TILE, axis=1)
        valid = valid[
            2 * TILE - row_halo : 2 * TILE + rows + row_halo,
            2 * TILE - col_halo : 2 * TILE + cols + col_halo,
        ]
        bias = jnp.where(to_groups(valid, dil) > 0.5, 0.0, NEG).astype(BF16)
        bias = jnp.broadcast_to(bias[..., None], bias.shape + (128,))
        own_rows = rows // dil * TILE
        bias_own = bias[:, 1:-1, REACH * TILE : REACH * TILE + own_rows].reshape(-1, 128)
        x_own = to_groups(x, dil).reshape(-1, WIDTH)
        stats = joined(register_stats(x_own, g, bias_own, w))
        keys = to_groups(extended(x, (row_halo, col_halo)), dil)
        x = from_groups(token_layer(keys, bias, g, w), dil, rows, cols)
        g = finish_registers(stats, g, w)
    return x, g


def solution(mesh):
    return jax.shard_map(
        shards,
        mesh=mesh,
        in_specs=(P("row", "col", None), P(), P("row", "col"), P(), P(), P(), P(), P(), P()),
        out_specs=(P("row", "col", None), P()),
        check_vma=False,
    )
```

time: 834 us -> 280 us (0.34); the launches traced: 818 us -> 279 us
  local copies, waits for them, and re-layouts: 328 us -> 33.8 us
  blocking collectives: 154 us -> 0 us
  Pallas kernels: 0 us -> 153 us
  matrix products: 133 us -> 0 us
  other arithmetic: 112 us -> 11.4 us
  between operations: 16.2 us -> 1.12 us
  waiting for transfers between devices: 18.8 us -> 28.6 us
    dynamic_slice x218 -> x0, local copies, waits for them, and re-layouts: 173 us -> none  [the longest x90 114 us: gather_neighbour_block(): lax.map(one, (query_tiles.reshape((count // group, group) + query_tiles.s...]
    all_gather x4 -> x0, blocking collectives: 154 us -> none  [joined(): gathered = jax.tree.map(lambda a: lax.all_gather(a, axis), part)]
    pallas_call x0 -> x6, Pallas kernels: none -> 153 us  [the longest x2 126 us: token_layer(): pl.pallas_call(layer_kernel, out_shape=jax.ShapeDtypeStruct(own, BF16), s...]
    dot_general x92 -> x0, matrix products: 133 us -> none  [the longest x18 70.2 us: tile_attention(): jnp.einsum('thqk,tkhe->tqhe', near_w.astype(jnp.bfloat16), v4, preferred_...]
    reduce_sum x50 -> x0, other arithmetic: 45.6 us -> none  [the longest x36 31.7 us: tile_attention(): total = jnp.sum(near_w, axis=-1) + jnp.sum(far_w, axis=-1)]
    slice x23 -> x10, local copies, waits for them, and re-layouts: 37.6 us -> 3.45 us  [the longest x1 2.01 us: layer_weights(): w_qkv[l, :, 2 * WIDTH:]]
    another operation x22 -> x1, local copies, waits for them, and re-layouts: 27.8 us -> 0.5 us  [to_groups(): x = x.reshape((rows // dil, dil, cols // (dil * TILE), TILE, dil) + rest)]
    add x145 -> x0, other arithmetic: 26.2 us -> none  [the longest x62 22.3 us: combine_stats(): first[1] * fa + second[1] * fb]
  transfers between devices with their start and end apart: 18 -> 22, of which waited for: 4 -> 10; matrix products, arithmetic and copies ran while one was open for 53% -> 8% of each run, Pallas kernels for 0% -> 24%
where the time goes in v1:
time: 280 us; the launch traced here: 279 us
  Pallas kernels  153 us (55%)
  starting transfers between devices  50.8 us (18%)
  local copies, waits for them, and re-layouts  33.8 us (12%)
  waiting for transfers between devices  28.6 us (10%)
  other arithmetic  11.4 us (4%)
    pallas_call x2, Pallas kernels, token_layer(): pl.pallas_call(layer_kernel, out_shape=jax.ShapeDtypeStruct(own, BF16), s...  126 us
    ppermute x6, starting transfers between devices, extended(): lax.ppermute(lax.slice_in_dim(block, size - width, size, axis=dim), axis,...  29.3 us
    pallas_call x2, Pallas kernels, register_stats(): pl.pallas_call(stats_kernel, out_shape=jax.ShapeDtypeStruct((HEAD + 8, HE...  19.2 us
    ppermute x6, waiting for transfers between devices, extended(): lax.ppermute(lax.slice_in_dim(block, 0, width, axis=dim), axis, backward)  15.5 us
    ppermute x10, waiting for transfers between devices, joined(): other = lax.ppermute(stats, axis, [(i, i ^ step) for i in range(count)])  12.7 us
    ppermute x10, starting transfers between devices, joined(): other = lax.ppermute(stats, axis, [(i, i ^ step) for i in range(count)])  11.8 us
    ppermute x6, starting transfers between devices, extended(): lax.ppermute(lax.slice_in_dim(block, 0, width, axis=dim), axis, backward)  9.64 us
    pallas_call x2, Pallas kernels, finish_registers(): pl.pallas_call(finish_kernel, out_shape=jax.ShapeDtypeStruct(g.shape, BF1...  7.36 us
  transfers between devices with their start and end apart: 22, of which 10 were waited for; matrix products, arithmetic and copies ran while one was open for 8% of the time, Pallas kernels for 24%

profile of v1, /device:TPU:1, one launch (start us, length us, event | category | flops | bytes accessed | tf_op | source)
XLA Modules:
  0.0 278.6 jit_solution(12611938640504261629)
XLA Ops:
  1.5 4.0 %collective-permute-start.4 = (bf16[2,6]{1,0:T(2,128)(2,1)S(1)}, bf16[2,6]{1,0:T(2,128)(2,1)S(1)}, u32[]{:S(2)}, u32[]{:S(2)}) collective-permute-start(bf16[2,6]{1,0:T(2,128)(2,1)S(1)} %get-tuple-element.50), channel_id=1, source_target_pairs={{0,8},{8,16},{16,24},{1,9},{9,17},{17,25},{2,10},{10,18},{18,26},{... | collective-permute-start | bytes 80 | tf_op jit(solution)/shard_map/ppermute | solution.py:313
  7.8 4.0 %collective-permute-start = (bf16[6,48,256]{2,1,0:T(8,128)(2,1)S(1)}, bf16[6,48,256]{2,1,0:T(8,128)(2,1)S(1)}, u32[]{:S(2)}, u32[]{:S(2)}) collective-permute-start(bf16[6,48,256]{2,1,0:T(8,128)(2,1)S(1)} %get-tuple-element.31), channel_id=1, source_target_pairs={{0,8},{8,16},{16,24},{1,9},{9,17},{17,25},{2,10},{10,18},{18,26},{... | collective-permute-start | bytes 442376 | tf_op jit(solution)/shard_map/ppermute | solution.py:313
  22.3 4.5 %collective-permute-start.6 = (bf16[10,2]{1,0:T(8,128)(2,1)S(1)}, bf16[10,2]{1,0:T(8,128)(2,1)S(1)}, u32[]{:S(2)}, u32[]{:S(2)}) collective-permute-start(bf16[10,2]{1,0:T(8,128)(2,1)S(1)} %get-tuple-element.44), channel_id=1, source_target_pairs={{0,1},{1,2},{2,3},{3,4},{4,5},{5,6},{6,7},{8,9},{9,10},{10,11},{11... | collective-permute-start | bytes 128 | tf_op jit(solution)/shard_map/ppermute | solution.py:313
  28.8 3.0 %collective-permute-done.7 = bf16[10,2]{1,0:T(8,128)(2,1)S(1)} collective-permute-done((bf16[10,2]{1,0:T(8,128)(2,1)S(1)}, bf16[10,2]{1,0:T(8,128)(2,1)S(1)}, u32[]{:S(2)}, u32[]{:S(2)}) %collective-permute-start.7) | collective-permute-done | bytes 72 | tf_op jit(solution)/shard_map/ppermute | solution.py:316
  33.8 9.6 %register_stats.2 = f32[40,512]{1,0:T(8,128)} custom-call(bf16[2304,256]{1,0:T(8,128)(2,1)} %bitcast.108, bf16[64,256]{1,0:T(8,128)(2,1)} %g_ref.5, bf16[2304,128]{1,0:T(8,128)(2,1)} %broadcast_in_dim.132.bias_ref, bf16[256,256]{1,0:T(8,128)(2,1)} %get-tuple-element.39.wq_ref, bf16[256,256]{1,0:T(8,128)(2,1)} %get-tuple-element.38.wk_ref, ...), custom_call_target="tpu_custom_call" | custom-call | tf_op jit(solution)/shard_map/register_stats/pallas_call | solution.py:242
  50.7 3.2 %collective-permute-done.14 = f32[40,512]{1,0:T(8,128)S(1)} collective-permute-done((f32[40,512]{1,0:T(8,128)S(1)}, f32[40,512]{1,0:T(8,128)S(1)}, u32[]{:S(2)}, u32[]{:S(2)}) %collective-permute-start.14) | collective-permute-done | bytes 81952 | tf_op jit(solution)/shard_map/ppermute | solution.py:301
  54.0 2.4 collective-permute-start.15
  56.4 5.9 %collective-permute-start.2 = (bf16[60,8,256]{2,1,0:T(8,128)(2,1)S(1)}, bf16[60,8,256]{2,1,0:T(8,128)(2,1)S(1)}, u32[]{:S(2)}, u32[]{:S(2)}) collective-permute-start(bf16[60,8,256]{2,1,0:T(8,128)(2,1)S(1)} %get-tuple-element.24), channel_id=1, source_target_pairs={{0,1},{1,2},{2,3},{3,4},{4,5},{5,6},{6,7},{8,9},{9,10},{10,11},{11... | collective-permute-start | bytes 737288 | tf_op jit(solution)/shard_map/ppermute | solution.py:313
  67.3 2.5 collective-permute-done.3
  72.8 52.5 %token_layer.2 = bf16[1,6,384,256]{3,2,1,0:T(8,128)(2,1)} custom-call(bf16[1,8,480,256]{3,2,1,0:T(8,128)(2,1)} %copy_bitcast_fusion.x_ref, bf16[1,8,480,128]{3,2,1,0:T(8,128)(2,1)} %broadcast_in_dim.125.bias_ref, bf16[64,256]{1,0:T(8,128)(2,1)} %g_ref.5, bf16[256,256]{1,0:T(8,128)(2,1)} %get-tuple-element.39.wq_ref, ...), custom_call_target="tpu_custom_call" | custom-call | tf_op jit(solution)/shard_map/token_layer/pallas_call | solution.py:268
  131.7 3.7 %finish_registers.2.g_ref = bf16[64,256]{1,0:T(8,128)(2,1)} custom-call(f32[40,512]{1,0:T(8,128)} %add_select_fusion.5.stats_ref, bf16[64,256]{1,0:T(8,128)(2,1)} %g_ref.5, bf16[256,256]{1,0:T(8,128)(2,1)} %get-tuple-element.39.wq_ref, bf16[256,256]{1,0:T(8,128)(2,1)} %get-tuple-element.38.wk_ref, bf16[256,256]{1,0:T(8,128)(2,1)} %bitcast.116, ...), custom_call_target="tpu_custom_call" | custom-call | tf_op jit(solution)/shard_map/finish_registers/pallas_call | solution.py:255
  136.5 9.6 %register_stats.3 = f32[40,512]{1,0:T(8,128)} custom-call(bf16[2304,256]{1,0:T(8,128)(2,1)} %bitcast.109, bf16[64,256]{1,0:T(8,128)(2,1)} %finish_registers.2.g_ref, bf16[2304,128]{1,0:T(8,128)(2,1)} %broadcast_in_dim.144.bias_ref, bf16[256,256]{1,0:T(8,128)(2,1)} %get-tuple-element.40.wq_ref, bf16[256,256]{1,0:T(8,128)(2,1)} %get-tuple-element.41.wk_ref, ...), custom_call_target="tpu_custom_call" | custom-call | tf_op jit(solution)/shard_map/register_stats/pallas_call | solution.py:242
  151.0 2.5 collective-permute-done.18
  153.7 3.3 %collective-permute-done.19 = f32[40,512]{1,0:T(8,128)S(1)} collective-permute-done((f32[40,512]{1,0:T(8,128)S(1)}, f32[40,512]{1,0:T(8,128)S(1)}, u32[]{:S(2)}, u32[]{:S(2)}) %collective-permute-start.19) | collective-permute-done | bytes 81952 | tf_op jit(solution)/shard_map/ppermute | solution.py:301
  157.1 3.5 %collective-permute-start.8 = (bf16[12,48,256]{2,1,0:T(8,128)(2,1)S(1)}, bf16[12,48,256]{2,1,0:T(8,128)(2,1)S(1)}, u32[]{:S(2)}, u32[]{:S(2)}) collective-permute-start(bf16[12,48,256]{2,1,0:T(8,128)(2,1)S(1)} %get-tuple-element.26), channel_id=1, source_target_pairs={{0,8},{8,16},{16,24},{1,9},{9,17},{17,25},{2,10},{10,18},{18,26},{... | collective-permute-start | bytes 884744 | tf_op jit(solution)/shard_map/ppermute | solution.py:313
  162.1 3.2 %collective-permute-start.21 = (f32[40,512]{1,0:T(8,128)S(1)}, f32[40,512]{1,0:T(8,128)S(1)}, u32[]{:S(2)}, u32[]{:S(2)}) collective-permute-start(f32[40,512]{1,0:T(8,128)S(1)} %add_select_fusion.1), channel_id=1, source_target_pairs={{0,16},{8,24},{16,0},{24,8},{1,17},{9,25},{17,1},{25,9},{2,18},{10... | collective-permute-start | bytes 245768 | tf_op jit(solution)/shard_map/ppermute | solution.py:301
  165.3 3.3 %collective-permute-done.9 = bf16[12,48,256]{2,1,0:T(8,128)(2,1)S(1)} collective-permute-done((bf16[12,48,256]{2,1,0:T(8,128)(2,1)S(1)}, bf16[12,48,256]{2,1,0:T(8,128)(2,1)S(1)}, u32[]{:S(2)}, u32[]{:S(2)}) %collective-permute-start.9) | collective-permute-done | bytes 294944 | tf_op jit(solution)/shard_map/ppermute | solution.py:316
  168.7 7.4 %collective-permute-start.10 = (bf16[72,16,256]{2,1,0:T(8,128)(2,1)S(1)}, bf16[72,16,256]{2,1,0:T(8,128)(2,1)}, u32[]{:S(2)}, u32[]{:S(2)}) collective-permute-start(bf16[72,16,256]{2,1,0:T(8,128)(2,1)S(1)} %get-tuple-element.22), channel_id=1, source_target_pairs={{0,1},{1,2},{2,3},{3,4},{4,5},{5,6},{6,7},{8,9},{9,10},{10,11},{11... | collective-permute-start | bytes 1769480 | tf_op jit(solution)/shard_map/ppermute | solution.py:313
  178.8 3.7 %finish_registers.3 = bf16[64,256]{1,0:T(8,128)(2,1)} custom-call(f32[40,512]{1,0:T(8,128)} %add_select_fusion.stats_ref, bf16[64,256]{1,0:T(8,128)(2,1)} %finish_registers.2.g_ref, bf16[256,256]{1,0:T(8,128)(2,1)} %get-tuple-element.40.wq_ref, bf16[256,256]{1,0:T(8,128)(2,1)} %get-tuple-element.41.wk_ref, bf16[256,256]{1,0:T(8,128)(2,1)} %bitcast.112, ...), custom_call_target="tpu_custom_call" | custom-call | tf_op jit(solution)/shard_map/finish_registers/pallas_call | solution.py:255
  182.9 6.7 %collective-permute-done.11 = bf16[72,16,256]{2,1,0:T(8,128)(2,1)} collective-permute-done((bf16[72,16,256]{2,1,0:T(8,128)(2,1)S(1)}, bf16[72,16,256]{2,1,0:T(8,128)(2,1)}, u32[]{:S(2)}, u32[]{:S(2)}) %collective-permute-start.11) | collective-permute-done | bytes 589856 | tf_op jit(solution)/shard_map/ppermute | solution.py:316
  191.5 3.1 %reshape.103 = bf16[36,2,5,8,2,256]{5,4,3,2,1,0:T(2,128)(2,1)} reshape(bf16[72,80,256]{2,1,0:T(8,128)(2,1)S(1)} %pad_maximum_fusion) | data formatting | bytes 5898240 | tf_op jit(solution)/shard_map/reshape | solution.py:324
  194.7 3.9 %copy.48 = bf16[2,2,5,36,8,256]{5,4,3,2,1,0:T(8,128)(2,1)} copy(bf16[2,2,5,36,8,256]{5,1,4,2,0,3:T(2,128)(2,1)} %bitcast.105) | data formatting | bytes 5898240 | tf_op jit(solution)/shard_map/transpose | solution.py:325
  200.3 73.9 %token_layer.3 = bf16[4,3,192,256]{3,2,1,0:T(8,128)(2,1)} custom-call(bf16[4,5,288,256]{3,2,1,0:T(8,128)(2,1)} %bitcast.104, bf16[4,5,288,128]{3,2,1,0:T(8,128)(2,1)} %broadcast_in_dim.130.bias_ref, bf16[64,256]{1,0:T(8,128)(2,1)} %finish_registers.2.g_ref, bf16[256,256]{1,0:T(8,128)(2,1)} %get-tuple-element.40.wq_ref, ...), custom_call_target="tpu_custom_call" | custom-call | tf_op jit(solution)/shard_map/token_layer/pallas_call | solution.py:268
  274.3 3.1 %copy.54 = bf16[24,2,3,8,2,256]{5,4,3,2,1,0:T(2,128)(2,1)S(1)} copy(bf16[24,2,3,8,2,256]{5,3,0,2,4,1:T(8,128)(2,1)} %bitcast.110) | data formatting | bytes 2359296 | tf_op jit(solution)/shard_map/transpose | solution.py:331
  (131 shorter events, 55.1 us)
Async XLA Ops:
  1.5 20.8 %collective-permute-start.4 = (bf16[2,6]{1,0:T(2,128)(2,1)S(1)}, bf16[2,6]{1,0:T(2,128)(2,1)S(1)}, u32[]{:S(2)}, u32[]{:S(2)}) collective-permute-start(bf16[2,6]{1,0:T(2,128)(2,1)S(1)} %get-tuple-element.50), channel_id=1, source_target_pairs={{0,8},{8,16},{16,24},{1,9},{9,17},{17,25},{2,10},{10,18},{18,26},{... | collective-permute-start | bytes 80 | tf_op jit(solution)/shard_map/ppermute | solution.py:313
  5.5 16.8 %collective-permute-start.5 = (bf16[2,6]{1,0:T(2,128)(2,1)S(1)}, bf16[2,6]{1,0:T(2,128)(2,1)S(1)}, u32[]{:S(2)}, u32[]{:S(2)}) collective-permute-start(bf16[2,6]{1,0:T(2,128)(2,1)S(1)} %get-tuple-element.51), channel_id=1, source_target_pairs={{8,0},{16,8},{24,16},{9,1},{17,9},{25,17},{10,2},{18,10},{26,18},{... | collective-permute-start | bytes 80 | tf_op jit(solution)/shard_map/ppermute | solution.py:316
  7.8 40.4 %collective-permute-start = (bf16[6,48,256]{2,1,0:T(8,128)(2,1)S(1)}, bf16[6,48,256]{2,1,0:T(8,128)(2,1)S(1)}, u32[]{:S(2)}, u32[]{:S(2)}) collective-permute-start(bf16[6,48,256]{2,1,0:T(8,128)(2,1)S(1)} %get-tuple-element.31), channel_id=1, source_target_pairs={{0,8},{8,16},{16,24},{1,9},{9,17},{17,25},{2,10},{10,18},{18,26},{... | collective-permute-start | bytes 442376 | tf_op jit(solution)/shard_map/ppermute | solution.py:313
  11.8 39.0 %collective-permute-start.1 = (bf16[6,48,256]{2,1,0:T(8,128)(2,1)S(1)}, bf16[6,48,256]{2,1,0:T(8,128)(2,1)S(1)}, u32[]{:S(2)}, u32[]{:S(2)}) collective-permute-start(bf16[6,48,256]{2,1,0:T(8,128)(2,1)S(1)} %get-tuple-element.30), channel_id=1, source_target_pairs={{8,0},{16,8},{24,16},{9,1},{17,9},{25,17},{10,2},{18,10},{26,18},{... | collective-permute-start | bytes 442376 | tf_op jit(solution)/shard_map/ppermute | solution.py:316
  13.1 51.2 %copy-start.6 = (pred[40]{0:T(512)(128)(4,1)}, pred[40]{0:T(512)(128)(4,1)S(1)}, u32[]{:S(2)}) copy-start(pred[40]{0:T(512)(128)(4,1)S(1)} %iota_compare_fusion) | copy-start | bytes 124
  22.3 6.4 %collective-permute-start.6 = (bf16[10,2]{1,0:T(8,128)(2,1)S(1)}, bf16[10,2]{1,0:T(8,128)(2,1)S(1)}, u32[]{:S(2)}, u32[]{:S(2)}) collective-permute-start(bf16[10,2]{1,0:T(8,128)(2,1)S(1)} %get-tuple-element.44), channel_id=1, source_target_pairs={{0,1},{1,2},{2,3},{3,4},{4,5},{5,6},{6,7},{8,9},{9,10},{10,11},{11... | collective-permute-start | bytes 128 | tf_op jit(solution)/shard_map/ppermute | solution.py:313
  26.9 4.9 %collective-permute-start.7 = (bf16[10,2]{1,0:T(8,128)(2,1)S(1)}, bf16[10,2]{1,0:T(8,128)(2,1)S(1)}, u32[]{:S(2)}, u32[]{:S(2)}) collective-permute-start(bf16[10,2]{1,0:T(8,128)(2,1)S(1)} %get-tuple-element.45), channel_id=1, source_target_pairs={{1,0},{2,1},{3,2},{4,3},{5,4},{6,5},{7,6},{9,8},{10,9},{11,10},{12... | collective-permute-start | bytes 128 | tf_op jit(solution)/shard_map/ppermute | solution.py:316
  43.4 2.5 collective-permute-start.12
  46.1 4.4 %collective-permute-start.13 = (f32[40,512]{1,0:T(8,128)S(1)}, f32[40,512]{1,0:T(8,128)S(1)}, u32[]{:S(2)}, u32[]{:S(2)}) collective-permute-start(f32[40,512]{1,0:T(8,128)S(1)} %add_select_fusion.9), channel_id=1, source_target_pairs={{0,2},{1,3},{2,0},{3,1},{4,6},{5,7},{6,4},{7,5},{8,10},{9,11},{10,... | collective-permute-start | bytes 245768 | tf_op jit(solution)/shard_map/ppermute | solution.py:301
  50.6 3.3 %collective-permute-start.14 = (f32[40,512]{1,0:T(8,128)S(1)}, f32[40,512]{1,0:T(8,128)S(1)}, u32[]{:S(2)}, u32[]{:S(2)}) collective-permute-start(f32[40,512]{1,0:T(8,128)S(1)} %add_select_fusion.8), channel_id=1, source_target_pairs={{0,4},{1,5},{2,6},{3,7},{4,0},{5,1},{6,2},{7,3},{8,12},{9,13},{10,... | collective-permute-start | bytes 245768 | tf_op jit(solution)/shard_map/ppermute | solution.py:301
  54.0 10.2 %collective-permute-start.15 = (f32[40,512]{1,0:T(8,128)S(1)}, f32[40,512]{1,0:T(8,128)S(1)}, u32[]{:S(2)}, u32[]{:S(2)}) collective-permute-start(f32[40,512]{1,0:T(8,128)S(1)} %add_select_fusion.7), channel_id=1, source_target_pairs={{0,8},{8,0},{16,24},{24,16},{1,9},{9,1},{17,25},{25,17},{2,10},{10... | collective-permute-start | bytes 245768 | tf_op jit(solution)/shard_map/ppermute | solution.py:301
  56.4 10.9 %collective-permute-start.2 = (bf16[60,8,256]{2,1,0:T(8,128)(2,1)S(1)}, bf16[60,8,256]{2,1,0:T(8,128)(2,1)S(1)}, u32[]{:S(2)}, u32[]{:S(2)}) collective-permute-start(bf16[60,8,256]{2,1,0:T(8,128)(2,1)S(1)} %get-tuple-element.24), channel_id=1, source_target_pairs={{0,1},{1,2},{2,3},{3,4},{4,5},{5,6},{6,7},{8,9},{9,10},{10,11},{11... | collective-permute-start | bytes 737288 | tf_op jit(solution)/shard_map/ppermute | solution.py:313
  62.3 7.5 %collective-permute-start.3 = (bf16[60,8,256]{2,1,0:T(8,128)(2,1)S(1)}, bf16[60,8,256]{2,1,0:T(8,128)(2,1)S(1)}, u32[]{:S(2)}, u32[]{:S(2)}) collective-permute-start(bf16[60,8,256]{2,1,0:T(8,128)(2,1)S(1)} %get-tuple-element.25), channel_id=1, source_target_pairs={{1,0},{2,1},{3,2},{4,3},{5,4},{6,5},{7,6},{9,8},{10,9},{11,10},{12... | collective-permute-start | bytes 737288 | tf_op jit(solution)/shard_map/ppermute | solution.py:316
  65.0 63.5 %collective-permute-start.16 = (f32[40,512]{1,0:T(8,128)}, f32[40,512]{1,0:T(8,128)}, u32[]{:S(2)}, u32[]{:S(2)}) collective-permute-start(f32[40,512]{1,0:T(8,128)} %add_select_fusion.6), channel_id=1, source_target_pairs={{0,16},{8,24},{16,0},{24,8},{1,17},{9,25},{17,1},{25,9},{2,18},{10... | collective-permute-start | bytes 245768 | tf_op jit(solution)/shard_map/ppermute | solution.py:301
  126.7 41.8 %copy-start = (bf16[48,48,256]{2,1,0:T(8,128)(2,1)}, bf16[48,48,256]{2,1,0:T(8,128)(2,1)S(1)}, u32[]{:S(2)}) copy-start(bf16[48,48,256]{2,1,0:T(8,128)(2,1)S(1)} %get-tuple-element.28) | copy-start | bytes 3538948
  146.1 1.5 collective-permute-start.17
  149.3 4.2 %collective-permute-start.18 = (f32[40,512]{1,0:T(8,128)S(1)}, f32[40,512]{1,0:T(8,128)S(1)}, u32[]{:S(2)}, u32[]{:S(2)}) collective-permute-start(f32[40,512]{1,0:T(8,128)S(1)} %add_select_fusion.4), channel_id=1, source_target_pairs={{0,2},{1,3},{2,0},{3,1},{4,6},{5,7},{6,4},{7,5},{8,10},{9,11},{10,... | collective-permute-start | bytes 245768 | tf_op jit(solution)/shard_map/ppermute | solution.py:301
  153.6 3.3 %collective-permute-start.19 = (f32[40,512]{1,0:T(8,128)S(1)}, f32[40,512]{1,0:T(8,128)S(1)}, u32[]{:S(2)}, u32[]{:S(2)}) collective-permute-start(f32[40,512]{1,0:T(8,128)S(1)} %add_select_fusion.3), channel_id=1, source_target_pairs={{0,4},{1,5},{2,6},{3,7},{4,0},{5,1},{6,2},{7,3},{8,12},{9,13},{10,... | collective-permute-start | bytes 245768 | tf_op jit(solution)/shard_map/ppermute | solution.py:301
  157.0 4.9 %collective-permute-start.20 = (f32[40,512]{1,0:T(8,128)S(1)}, f32[40,512]{1,0:T(8,128)S(1)}, u32[]{:S(2)}, u32[]{:S(2)}) collective-permute-start(f32[40,512]{1,0:T(8,128)S(1)} %add_select_fusion.2), channel_id=1, source_target_pairs={{0,8},{8,0},{16,24},{24,16},{1,9},{9,1},{17,25},{25,17},{2,10},{10... | collective-permute-start | bytes 245768 | tf_op jit(solution)/shard_map/ppermute | solution.py:301
  157.1 8.2 %collective-permute-start.8 = (bf16[12,48,256]{2,1,0:T(8,128)(2,1)S(1)}, bf16[12,48,256]{2,1,0:T(8,128)(2,1)S(1)}, u32[]{:S(2)}, u32[]{:S(2)}) collective-permute-start(bf16[12,48,256]{2,1,0:T(8,128)(2,1)S(1)} %get-tuple-element.26), channel_id=1, source_target_pairs={{0,8},{8,16},{16,24},{1,9},{9,17},{17,25},{2,10},{10,18},{18,26},{... | collective-permute-start | bytes 884744 | tf_op jit(solution)/shard_map/ppermute | solution.py:313
  160.7 7.9 %collective-permute-start.9 = (bf16[12,48,256]{2,1,0:T(8,128)(2,1)S(1)}, bf16[12,48,256]{2,1,0:T(8,128)(2,1)S(1)}, u32[]{:S(2)}, u32[]{:S(2)}) collective-permute-start(bf16[12,48,256]{2,1,0:T(8,128)(2,1)S(1)} %get-tuple-element.27), channel_id=1, source_target_pairs={{8,0},{16,8},{24,16},{9,1},{17,9},{25,17},{10,2},{18,10},{26,18},{... | collective-permute-start | bytes 884744 | tf_op jit(solution)/shard_map/ppermute | solution.py:316
  162.1 15.9 %collective-permute-start.21 = (f32[40,512]{1,0:T(8,128)S(1)}, f32[40,512]{1,0:T(8,128)S(1)}, u32[]{:S(2)}, u32[]{:S(2)}) collective-permute-start(f32[40,512]{1,0:T(8,128)S(1)} %add_select_fusion.1), channel_id=1, source_target_pairs={{0,16},{8,24},{16,0},{24,8},{1,17},{9,25},{17,1},{25,9},{2,18},{10... | collective-permute-start | bytes 245768 | tf_op jit(solution)/shard_map/ppermute | solution.py:301
  168.7 14.2 %collective-permute-start.10 = (bf16[72,16,256]{2,1,0:T(8,128)(2,1)S(1)}, bf16[72,16,256]{2,1,0:T(8,128)(2,1)}, u32[]{:S(2)}, u32[]{:S(2)}) collective-permute-start(bf16[72,16,256]{2,1,0:T(8,128)(2,1)S(1)} %get-tuple-element.22), channel_id=1, source_target_pairs={{0,1},{1,2},{2,3},{3,4},{4,5},{5,6},{6,7},{8,9},{9,10},{10,11},{11... | collective-permute-start | bytes 1769480 | tf_op jit(solution)/shard_map/ppermute | solution.py:313
  176.1 13.5 %collective-permute-start.11 = (bf16[72,16,256]{2,1,0:T(8,128)(2,1)S(1)}, bf16[72,16,256]{2,1,0:T(8,128)(2,1)}, u32[]{:S(2)}, u32[]{:S(2)}) collective-permute-start(bf16[72,16,256]{2,1,0:T(8,128)(2,1)S(1)} %get-tuple-element.23), channel_id=1, source_target_pairs={{1,0},{2,1},{3,2},{4,3},{5,4},{6,5},{7,6},{9,8},{10,9},{11,10},{12... | collective-permute-start | bytes 1769480 | tf_op jit(solution)/shard_map/ppermute | solution.py:316
  (9 other events, 50.1 us)

commit v2 on v1

v2 whole, which is shorter than its diff:
```python
import math

import jax
import jax.numpy as jnp
from jax import lax
from jax.experimental import pallas as pl
from jax.experimental.pallas import tpu as pltpu
from jax.sharding import PartitionSpec as P

HEADS = 8
HEAD = 32
WIDTH = 256
REGS = 64
TILE = 8
LAYERS = 2
DILATIONS = (1, 2)
REACH = 6
QROWS = 4
KROWS = QROWS + 2 * REACH
GKEYS = KROWS * TILE
KEYS = 3 * GKEYS
QTILE = QROWS * TILE
RIM = REACH * TILE
CHUNK = 384
ONES = 16
UNITS = 8
NEG = -1e30
BIG = 1e30
LIMIT = 2.0**100
EPS = 1e-05
SCALE = math.log2(math.e) * HEAD**-0.5
F32 = jnp.float32
BF16 = jnp.bfloat16


def mm(a, b):
    return lax.dot_general(a, b, (((1,), (0,)), ((), ())), preferred_element_type=F32)


def mm_nt(a, b):
    return lax.dot_general(a, b, (((1,), (1,)), ((), ())), preferred_element_type=F32)


def normed(x, gain):
    v = x.astype(F32)
    mean = jnp.mean(v, axis=-1, keepdims=True)
    centred = v - mean
    spread = jnp.mean(centred * centred, axis=-1, keepdims=True)
    return centred * lax.rsqrt(spread + EPS) * gain


def iota(shape, dim):
    return lax.broadcasted_iota(jnp.int32, shape, dim)


def ones_where(cond):
    return jnp.where(cond, 1.0, 0.0).astype(BF16)


def head_mask(rows_per_head):
    shape = (HEADS * rows_per_head, WIDTH)
    return ones_where(iota(shape, 0) // rows_per_head == iota(shape, 1) // HEAD)


def spread_heads(q, mask):
    return jnp.concatenate([q] * HEADS, axis=0) * mask


def twice(a):
    return jnp.concatenate([a, a], axis=1)


def first_lane():
    return ones_where(iota((ONES, 128), 1) == 0)


def diagonal(part):
    lane = iota((HEAD, WIDTH), 1) // REGS
    out = jnp.zeros((HEAD, WIDTH), F32)
    for b in range(WIDTH // REGS):
        out = out + jnp.where(lane == b, part[b * HEAD : (b + 1) * HEAD, :], 0.0)
    return out


def mlp(x, gain2, w_up, w_down):
    z = mm(normed(x, gain2).astype(BF16), w_up)
    slope = math.sqrt(2.0 / math.pi)
    u = (z + z * jnp.tanh(z * (slope + (slope * 0.044715) * (z * z)))).astype(BF16)
    return (x.astype(F32) + 0.5 * mm(u, w_down)).astype(BF16)


def block_valid(mask_ref, dil, group):
    rows = TILE * TILE // dil
    shape = (rows, 128)
    parts = []
    for r in range(mask_ref.shape[0]):
        if dil == 1:
            part = jnp.full(shape, mask_ref[r, group].astype(F32), F32)
        else:
            low = jnp.full(shape, mask_ref[r, 2 * group].astype(F32), F32)
            high = jnp.full(shape, mask_ref[r, 2 * group + 1].astype(F32), F32)
            part = jnp.where(iota(shape, 0) % TILE < TILE // 2, low, high)
        parts.append(part)
    return jnp.concatenate(parts, axis=0)


def own_kernel(
    dil, groups, x_ref, mask_ref, g_ref, wq_ref, wk_ref, wvt_ref, gain_ref,
    h_ref, k_ref, q_ref, v_ref, stats_ref, left_ref, right_ref, acc_ref, t_ref,
):
    gain = gain_ref[...]
    chunks = x_ref.shape[0] // CHUNK
    per_chunk = dil * dil * groups // chunks
    hg = normed(g_ref[...], gain).astype(BF16)
    rq_bd = spread_heads((mm(hg, wq_ref[...]) * SCALE).astype(BF16), head_mask(REGS))
    rk = mm(hg, wk_ref[...]).astype(BF16)
    shift = jnp.max(mm_nt(rk, rq_bd), axis=0, keepdims=True)
    lane = first_lane()
    acc_ref[...] = jnp.zeros_like(acc_ref)

    def accumulate(h, valid, w):
        vt = mm_nt(wvt_ref[...], h).astype(BF16)
        ones = mm_nt(lane, valid).astype(BF16)
        for a in range(2):
            lhs = jnp.concatenate([vt[128 * a : 128 * a + 128], ones], axis=0)
            acc_ref[a] += mm(lhs, w[:, WIDTH * a : WIDTH * (a + 1)])

    def chunk(n, carry):
        rows = pl.ds(pl.multiple_of(n * CHUNK, CHUNK), CHUNK)
        valid = jnp.concatenate(
            [
                block_valid(mask_ref, dil, lax.rem(n * per_chunk + p, groups))
                for p in range(per_chunk)
            ],
            axis=0,
        )
        h32 = normed(x_ref[rows, :], gain)
        q_ref[rows, :] = (mm(h32.astype(BF16), wq_ref[...]) * SCALE).astype(BF16)
        h = (h32 * twice(valid)).astype(BF16)
        valid = valid.astype(BF16)
        k = mm(h, wk_ref[...]).astype(BF16)
        h_ref[rows, :] = h
        k_ref[rows, :] = k
        v_ref[rows, :] = valid
        accumulate(h, valid, jnp.exp2(mm_nt(k, rq_bd) - shift).astype(BF16))
        return carry

    lax.fori_loop(0, chunks, chunk, 0, unroll=2)

    size = left_ref.shape[1]
    for gr in range(dil * dil):
        for ref, c in ((left_ref, 0), (right_ref, groups - 1)):
            rows = slice((gr * groups + c) * size, (gr * groups + c + 1) * size)
            live = twice(v_ref[rows, :].astype(F32)) > 0.5
            ref[gr] = jnp.where(live, x_ref[rows, :].astype(F32), BIG).astype(BF16)

    def write(top):
        n0, n1 = acc_ref[0], acc_ref[1]
        stats_ref[0:HEAD, :] = jnp.concatenate([diagonal(n0), diagonal(n1)], axis=1)
        total = jnp.concatenate([n0[128:136], n1[128:136]], axis=1)
        row = iota((8, 2 * WIDTH), 0)
        stats_ref[HEAD : HEAD + 8, :] = jnp.where(row == 0, top, jnp.where(row == 1, total, 0.0))

    write(shift)
    worst = jnp.max(jnp.where(acc_ref[:, 128:136, :] < LIMIT, 0.0, 1.0))

    @pl.when(worst > 0.5)
    def _():
        def scores(n, top):
            rows = pl.ds(pl.multiple_of(n * CHUNK, CHUNK), CHUNK)
            live = jnp.concatenate([v_ref[rows, :].astype(F32)] * 4, axis=1) > 0.5
            t = jnp.where(live, mm_nt(k_ref[rows, :], rq_bd), NEG)
            t_ref[rows, :] = t
            return jnp.maximum(top, jnp.max(t, axis=0, keepdims=True))

        top = lax.fori_loop(0, chunks, scores, jnp.full((1, 2 * WIDTH), NEG, F32))
        acc_ref[...] = jnp.zeros_like(acc_ref)

        def weigh(n, carry):
            rows = pl.ds(pl.multiple_of(n * CHUNK, CHUNK), CHUNK)
            w = jnp.exp2(t_ref[rows, :] - top).astype(BF16)
            accumulate(h_ref[rows, :], v_ref[rows, :], w)
            return carry

        lax.fori_loop(0, chunks, weigh, 0)
        write(top)


def finish_kernel(
    stats_ref, g_ref, wq_ref, wk_ref, wvt_ref, gain_ref, wo_ref, wu_ref, wd_ref, gain2_ref, out_ref
):
    g = g_ref[...]
    hg = normed(g, gain_ref[...]).astype(BF16)
    rq_bd = spread_heads((mm(hg, wq_ref[...]) * SCALE).astype(BF16), head_mask(REGS))
    rk = mm(hg, wk_ref[...]).astype(BF16)
    rvt = mm_nt(wvt_ref[...], hg).astype(BF16)
    own = mm_nt(rk, rq_bd)
    own_top = jnp.max(own, axis=0, keepdims=True)
    w = jnp.exp2(own - own_top)
    own_total = jnp.sum(w, axis=0, keepdims=True)
    wb = w.astype(BF16)
    own_numer = jnp.concatenate(
        [diagonal(mm(rvt[:128], wb[:, :WIDTH])), diagonal(mm(rvt[128:], wb[:, WIDTH:]))], axis=1
    )
    top = stats_ref[HEAD : HEAD + 1, :]
    total = stats_ref[HEAD + 1 : HEAD + 2, :]
    peak = jnp.maximum(top, own_top)
    keep = jnp.exp2(top - peak)
    keep_own = jnp.exp2(own_top - peak)
    total = total * keep + own_total * keep_own
    z = ((stats_ref[0:HEAD, :] * keep + own_numer * keep_own) / total).astype(BF16)
    shape = (WIDTH, HEADS * REGS)
    mask = ones_where(iota(shape, 0) // HEAD == iota(shape, 1) // REGS)
    z = jnp.concatenate([z] * HEADS, axis=0) * mask
    pick_shape = (REGS, HEADS * REGS)
    pick = ones_where(iota(pick_shape, 0) == iota(pick_shape, 1) % REGS)
    attended = mm_nt(pick, z).astype(BF16)
    g = (g.astype(F32) + mm(attended, wo_ref[...])).astype(BF16)
    out_ref[...] = mlp(g, gain2_ref[...], wu_ref[...], wd_ref[...])


def attend_kernel(dil, edges, *refs):
    (
        flags_ref, mask_in_ref, x_ref, h_ref, k_ref, q_ref, v_ref, top_ref, bottom_ref, g_ref,
        wk_ref, wvt_ref, gain_ref, wo_ref, wu_ref, wd_ref, gain2_ref,
    ) = refs[:17]
    refs = refs[17:]
    grids, own_groups, rows, _ = x_ref.shape
    strips = rows // QTILE
    if edges:
        left_ref, right_ref, middle_ref = refs[:3]
        outs, refs = (refs[3:6], refs[6:]) if dil == 1 else (refs[3:4], refs[4:])
        new_ref, refs = refs[0], refs[1:]
        sources = [None, 0, 1, own_groups - 2, own_groups - 1, None]
        tiles, tile_step, own_at, own_step = 2, 3, 0, own_groups - 1
    else:
        new_ref, refs = refs[0], refs[1:]
        sources = list(range(own_groups))
        tiles, tile_step, own_at, own_step = own_groups - 2, 1, 1, 1
    kh_ref, kk_ref, kv_ref, vt_ref, win_ref, head_ref, att_ref, chk_ref, w_ref, o_ref = refs
    at_once = vt_ref.shape[0] // grids
    groups = len(sources)
    gain = gain_ref[...]
    lane = first_lane()

    hg = normed(g_ref[...], gain).astype(BF16)
    rk = mm(hg, wk_ref[...]).astype(BF16)
    rvt = mm_nt(wvt_ref[...], hg).astype(BF16)
    ones = jnp.full((ONES, REGS), 1.0, BF16)
    rvts = [jnp.concatenate([rvt[128 * a : 128 * a + 128], ones], axis=0) for a in range(2)]
    head_ref[...] = head_mask(QTILE)
    shape = (KEYS, 128)
    key, query = iota(shape, 0), iota(shape, 1) % QTILE
    row_step = (key % GKEYS) // TILE - query // TILE
    col_step = (key // GKEYS - 1) * TILE + key % TILE - query % TILE
    win_ref[...] = ones_where(
        (row_step >= 0) & (row_step <= 2 * REACH) & (col_step >= -REACH) & (col_step <= REACH)
    )
    chk_ref[...] = jnp.zeros_like(chk_ref)

    has = [flags_ref[0, n].astype(F32) for n in range(4)]

    def from_rim(x, known):
        x = x.astype(F32)
        valid = jnp.where(jnp.abs(x[:, 0:1]) < 0.5 * BIG, 1.0, 0.0) * known
        h = (normed(jnp.where(valid > 0.5, x, 0.0), gain) * valid).astype(BF16)
        k = mm(h, wk_ref[...]).astype(BF16)
        return h, k, jnp.broadcast_to(valid, (x.shape[0], 128)).astype(BF16)

    held = [(c, source) for c, source in enumerate(sources) if source is not None]

    def assemble(gr, carry):
        for c, source in held:
            for ref, own in ((kh_ref, h_ref), (kk_ref, k_ref), (kv_ref, v_ref)):
                ref[gr, c, RIM : RIM + rows, :] = own[gr, source]
        x = [top_ref[gr, source] for _, source in held]
        x += [bottom_ref[gr, source] for _, source in held]
        size = len(held) * RIM
        known = jnp.where(iota((2 * size, 1), 0) < size, has[0], has[1])
        parts = from_rim(jnp.concatenate(x, axis=0), known)
        for n, (c, _) in enumerate(held):
            for ref, part in zip((kh_ref, kk_ref, kv_ref), parts):
                ref[gr, c, 0:RIM, :] = part[n * RIM : (n + 1) * RIM]
                ref[gr, c, RIM + rows :, :] = part[size + n * RIM : size + (n + 1) * RIM]
        if edges:
            size = rows + 2 * RIM
            row = iota((size, 1), 0)
            rim = jnp.where(row < RIM, has[0], jnp.where(row < RIM + rows, 1.0, has[1]))
            known = jnp.concatenate([rim * has[2], rim * has[3]], axis=0)
            parts = from_rim(jnp.concatenate([left_ref[gr], right_ref[gr]], axis=0), known)
            for n, c in ((0, 0), (1, groups - 1)):
                for ref, part in zip((kh_ref, kk_ref, kv_ref), parts):
                    ref[gr, c] = part[n * size : (n + 1) * size]
        return carry

    lax.fori_loop(0, grids, assemble, 0, unroll=min(grids, 2))

    half = (128, 128)
    diag = iota(half, 0) // HEAD == iota(half, 1) // QTILE
    pick_shape = (QTILE, 128)
    pick = ones_where(iota(pick_shape, 0) == iota(pick_shape, 1) % QTILE)

    def keys_of(i):
        start = pl.multiple_of(i * QTILE, QTILE)
        return pl.ds(start, QTILE), pl.ds(start, GKEYS)

    def values(slot, gr, i):
        _, key_at = keys_of(i)
        hs = kh_ref[gr, :, key_at, :].reshape(groups * GKEYS, WIDTH)
        vs = kv_ref[gr, :, key_at, :].reshape(groups * GKEYS, 128)
        vt_ref[slot, 0:WIDTH, :] = mm_nt(wvt_ref[...], hs).astype(BF16)
        vt_ref[slot, WIDTH:, :] = mm_nt(lane, vs).astype(BF16)

    def scores(gr, i, t):
        query_at, key_at = keys_of(i)
        q_bd = spread_heads(q_ref[gr, own_at + t * own_step, query_at, :], head_ref[...])
        k = kk_ref[gr, pl.ds(t * tile_step, 3), key_at, :].reshape(KEYS, WIDTH)
        return mm_nt(jnp.concatenate([rk, k], axis=0), q_bd)

    def weighted(u, slot, t):
        lanes = pl.ds(t * tile_step * GKEYS, KEYS)
        if not isinstance(t, int):
            lanes = pl.ds(pl.multiple_of(t * tile_step * GKEYS, GKEYS), KEYS)
        totals = []
        for a in range(2):
            vt = jnp.concatenate(
                [vt_ref[slot, 128 * a : 128 * a + 128, lanes], vt_ref[slot, WIDTH:, lanes]], axis=0
            )
            o = mm(
                jnp.concatenate([vt, rvts[a]], axis=1), w_ref[u, :, 128 * a : 128 * a + 128]
            )
            total = o[128:129]
            totals.append(total)
            o_ref[u, a] = jnp.where(diag, o[:128] * (1.0 / total), 0.0).astype(BF16)
        return jnp.concatenate(totals, axis=1)

    def turned(u, gr, i, t):
        query_at, _ = keys_of(i)
        parts = [mm_nt(pick, o_ref[u, a]) for a in range(2)]
        att_ref[gr, t, query_at, :] = jnp.concatenate(parts, axis=1).astype(BF16)

    def batch(n, carry):
        slots = [(gr, n * at_once + i) for i in range(at_once) for gr in range(grids)]
        units = [(slot, t) for slot in range(len(slots)) for t in range(tiles)]
        bad = jnp.zeros((1, WIDTH), F32)
        for step in range(len(units) + 2):
            if step < len(units):
                slot, t = units[step]
                if t == 0:
                    values(slot, *slots[slot])
                s = scores(*slots[slot], t)
                shift = jnp.max(s[:REGS], axis=0, keepdims=True)
                w = jnp.exp2(s - shift).astype(BF16)
                w_ref[step, KEYS:, :] = w[:REGS]
                w_ref[step, :KEYS, :] = w[REGS:] * twice(win_ref[...])
            if 0 <= step - 1 < len(units):
                slot, t = units[step - 1]
                total = weighted(step - 1, slot, t)
                bad = jnp.maximum(bad, jnp.where(total < LIMIT, 0.0, 1.0))
            if step >= 2:
                slot, t = units[step - 2]
                turned(step - 2, *slots[slot], t)
        chk_ref[0:1, :] = jnp.maximum(chk_ref[0:1, :], bad)
        return carry

    lax.fori_loop(0, strips // at_once, batch, 0)

    @pl.when(jnp.max(chk_ref[...]) > 0.5)
    def _():
        def again(n, carry):
            gr, i = n // strips, n % strips
            _, key_at = keys_of(i)
            values(0, gr, i)

            def tile(t, carry):
                s = scores(gr, i, t)
                valid = kv_ref[gr, pl.ds(t * tile_step, 3), key_at, :].reshape(KEYS, 128)
                live = twice((valid * win_ref[...]).astype(F32)) > 0.5
                live = jnp.concatenate([jnp.full((REGS, WIDTH), True), live], axis=0)
                s = jnp.where(live, s, NEG)
                top = jnp.max(s, axis=0, keepdims=True)
                w = jnp.where(live, jnp.exp2(s - top), 0.0).astype(BF16)
                w_ref[0, KEYS:, :] = w[:REGS]
                w_ref[0, :KEYS, :] = w[REGS:]
                weighted(0, 0, t)
                turned(0, gr, i, t)
                return carry

            return lax.fori_loop(0, tiles, tile, carry)

        lax.fori_loop(0, grids * strips, again, 0)

    def tail(n, carry):
        gr, t = n // tiles, n % tiles
        x = x_ref[gr, own_at + t * own_step]
        x = (x.astype(F32) + mm(att_ref[gr, t], wo_ref[...])).astype(BF16)
        new_ref[gr, t] = mlp(x, gain2_ref[...], wu_ref[...], wd_ref[...])
        return carry

    lax.fori_loop(0, grids * tiles, tail, 0, unroll=2)
    if not edges:
        return

    def group(gr, c, at):
        if c == 0:
            return new_ref[gr, 0, at, :]
        if c == own_groups - 1:
            return new_ref[gr, 1, at, :]
        return middle_ref[gr, c - 1, at, :]

    square = (128, 128)
    to, of = iota(square, 0), iota(square, 1)
    if dil == 1:
        out_ref, first_ref, last_ref = outs
        a, b = to // 64, (to // 32) % 2
        rr, cc = (to % 32) // TILE, to % TILE
        source = (cc // 4) * 64 + (2 * rr + a) * TILE + 2 * (cc % 4) + b
        perm = ones_where(of == source)
        for c in range(own_groups // 2):
            for r in range(rows // 64):
                at = slice(64 * r, 64 * r + 64)
                both = jnp.concatenate([group(0, 2 * c, at), group(0, 2 * c + 1, at)], axis=0)
                y = mm(perm, both).astype(BF16)
                for gr in range(4):
                    out_ref[gr, c, 32 * r : 32 * r + 32, :] = y[32 * gr : 32 * gr + 32]
            live = twice(block_valid(mask_in_ref, 2, c)) > 0.5
            size = live.shape[0]
            for gr in range(4):
                for ref, at in ((first_ref, slice(0, RIM)), (last_ref, slice(size - RIM, size))):
                    y = jnp.where(live[at], out_ref[gr, c, at, :].astype(F32), BIG)
                    ref[gr, c] = y.astype(BF16)
    else:
        (out_ref,) = outs
        r, col = to // 16, to % 16
        source = (2 * (r % 2) + col % 2) * 32 + (r // 2) * TILE + col // 2
        perm = ones_where(of == source)
        for c in range(own_groups):
            for r in range(rows // 32):
                at = slice(32 * r, 32 * r + 32)
                four = jnp.concatenate([group(gr, c, at) for gr in range(4)], axis=0)
                y = mm(perm, four).astype(BF16)
                for n in range(TILE):
                    out_ref[TILE * r + n, 16 * c : 16 * c + 16, :] = y[16 * n : 16 * n + 16]


VMEM = pl.BlockSpec(memory_space=pltpu.VMEM)
SMEM = pl.BlockSpec(memory_space=pltpu.SMEM)


def call(kernel, name, out_shape, scratch, specs, micros, *args):
    return pl.pallas_call(
        kernel,
        out_shape=out_shape,
        in_specs=specs,
        out_specs=jax.tree.map(lambda _: VMEM, out_shape),
        scratch_shapes=scratch,
        compiler_params=pltpu.CompilerParams(vmem_limit_bytes=40 * 1024 * 1024),
        cost_estimate=pl.CostEstimate(
            flops=micros * 10**9, transcendentals=0, bytes_accessed=micros * 10**6
        ),
        name=name,
    )(*args)


def shape(dims, dtype=BF16):
    return jax.ShapeDtypeStruct(dims, dtype)


def own_tokens(dil, x, mask, g, w):
    grids, groups, rows, _ = x.shape
    tokens = grids * groups * rows
    outs = call(
        lambda *refs: own_kernel(dil, groups, *refs),
        "own_tokens",
        [
            shape((tokens, WIDTH)),
            shape((tokens, WIDTH)),
            shape((tokens, WIDTH)),
            shape((tokens, 128)),
            shape((HEAD + 8, HEADS * REGS), F32),
            shape((grids, rows, WIDTH)),
            shape((grids, rows, WIDTH)),
        ],
        [
            pltpu.VMEM((2, 128 + ONES, WIDTH), F32),
            pltpu.VMEM((tokens, HEADS * REGS), F32),
        ],
        [VMEM, SMEM] + [VMEM] * 5,
        6,
        x.reshape(tokens, WIDTH), mask, g, w["q"], w["k"], w["vt"], w["gain"],
    )
    split = [a.reshape(grids, groups, rows, a.shape[-1]) for a in outs[:4]]
    return split, outs[4], outs[5], outs[6]


def finish_registers(stats, g, w):
    return call(
        finish_kernel, "finish_registers", shape(g.shape), [], [VMEM] * 10, 3,
        stats, g, w["q"], w["k"], w["vt"], w["gain"], w["out"], w["up"], w["down"], w["gain2"],
    )


def attend(dil, flags, mask, x, own, rims, g, w, sides=None):
    grids, groups, rows, _ = x.shape
    h, k, q, v = own
    edges = sides is not None
    tiles = 2 if edges else groups - 2
    held = 6 if edges else groups
    at_once = max(1, UNITS // (grids * tiles))
    new = (grids, tiles, rows, WIDTH)
    keys = (grids, held, rows + 2 * RIM)
    scratch = [
        pltpu.VMEM(keys + (WIDTH,), BF16),
        pltpu.VMEM(keys + (WIDTH,), BF16),
        pltpu.VMEM(keys + (128,), BF16),
        pltpu.VMEM((at_once * grids, WIDTH + ONES, held * GKEYS), BF16),
        pltpu.VMEM((KEYS, 128), BF16),
        pltpu.VMEM((HEADS * QTILE, WIDTH), BF16),
        pltpu.VMEM(new, BF16),
        pltpu.VMEM((8, WIDTH), F32),
        pltpu.VMEM((at_once * grids * tiles, KEYS + REGS, WIDTH), BF16),
        pltpu.VMEM((at_once * grids * tiles, 2, 128, 128), BF16),
    ]
    if not edges:
        out = shape(new)
    else:
        scratch = [pltpu.VMEM(new, BF16)] + scratch
        if dil == 1:
            after = (4, groups // 2, rows // 2)
            rim = (4, groups // 2, RIM, WIDTH)
            out = [shape(after + (WIDTH,)), shape(rim), shape(rim)]
        else:
            out = [shape((mask.shape[0] * TILE, mask.shape[1] * TILE, WIDTH))]
    args = (
        flags, mask, x, h, k, q, v, *rims, g,
        w["k"], w["vt"], w["gain"], w["out"], w["up"], w["down"], w["gain2"],
    ) + (tuple(sides) if edges else ())
    return call(
        lambda *refs: attend_kernel(dil, edges, *refs),
        "attend_edges" if edges else "attend_middle",
        out,
        scratch,
        [SMEM, SMEM] + [VMEM] * (len(args) - 2),
        12,
        *args,
    )


def combine(a, b):
    top_a, top_b = a[HEAD : HEAD + 1], b[HEAD : HEAD + 1]
    peak = jnp.maximum(top_a, top_b)
    fa, fb = jnp.exp2(top_a - peak), jnp.exp2(top_b - peak)
    out = a * fa + b * fb
    row = lax.broadcasted_iota(jnp.int32, out.shape, 0)
    return jnp.where(row == HEAD, peak, out)


def joined(stats):
    for axis in ("col", "row"):
        count = lax.axis_size(axis)
        step = 1
        while step < count:
            other = lax.ppermute(stats, axis, [(i, i ^ step) for i in range(count)])
            stats = combine(stats, other)
            step *= 2
    return stats


def exchanged(first, last, axis):
    count = lax.axis_size(axis)
    forward = [(i, i + 1) for i in range(count - 1)]
    backward = [(target, source) for source, target in forward]
    return lax.ppermute(last, axis, forward), lax.ppermute(first, axis, backward)


def to_groups(x):
    rows, cols = x.shape[:2]
    x = jnp.transpose(x.reshape(rows, cols // TILE, TILE, WIDTH), (1, 0, 2, 3))
    return x.reshape(1, cols // TILE, rows * TILE, WIDTH)


def layer_weights(l, w_qkv, w_out, w_up, w_down, norm_attn, norm_mlp):
    return {
        "q": w_qkv[l, :, :WIDTH],
        "k": w_qkv[l, :, WIDTH : 2 * WIDTH],
        "vt": w_qkv[l, :, 2 * WIDTH :].T,
        "out": w_out[l],
        "up": w_up[l],
        "down": w_down[l],
        "gain": norm_attn[l : l + 1],
        "gain2": norm_mlp[l : l + 1],
    }


def shards(tokens, registers, tile_mask, w_qkv, w_out, w_up, w_down, norm_attn, norm_mlp):
    places = [(lax.axis_index(axis), lax.axis_size(axis)) for axis in ("row", "col")]
    flags = jnp.stack([f for at, n in places for f in (at > 0, at < n - 1)])
    flags = flags.astype(jnp.int32).reshape(1, 4)

    def rim(x, mask_row):
        live = jnp.repeat(mask_row, TILE)[None, :, None] > 0
        return to_groups(jnp.where(live, x, jnp.asarray(BIG, BF16)))

    first, last = rim(tokens[:REACH], tile_mask[0]), rim(tokens[-REACH:], tile_mask[-1])
    x, g = to_groups(tokens), registers
    for l in range(LAYERS):
        dil = DILATIONS[l % 2]
        w = layer_weights(l, w_qkv, w_out, w_up, w_down, norm_attn, norm_mlp)
        top, bottom = exchanged(first, last, "row")
        own, stats, left_own, right_own = own_tokens(dil, x, tile_mask, g, w)
        stats = joined(stats)
        left_own = jnp.concatenate([top[:, 0], left_own, bottom[:, 0]], axis=1)
        right_own = jnp.concatenate([top[:, -1], right_own, bottom[:, -1]], axis=1)
        left, right = exchanged(left_own, right_own, "col")
        rims = (top, bottom)
        middle = attend(dil, flags, tile_mask, x, own, rims, g, w)
        out = attend(dil, flags, tile_mask, x, own, rims, g, w, (left, right, middle))
        g = finish_registers(stats, g, w)
        if l < LAYERS - 1:
            x, first, last = out
    return out[0], g


def solution(mesh):
    return jax.shard_map(
        shards,
        mesh=mesh,
        in_specs=(P("row", "col", None), P(), P("row", "col"), P(), P(), P(), P(), P(), P()),
        out_specs=(P("row", "col", None), P()),
        check_vma=False,
    )
```

time: 280 us -> 298 us (1.064)
  Pallas kernels: 153 us -> 234 us
  local copies, waits for them, and re-layouts: 33.8 us -> 11.9 us
  waiting for transfers between devices: 28.6 us -> 8.37 us
  starting transfers between devices: 50.8 us -> 38.4 us
  other arithmetic: 11.4 us -> 3.11 us
    pallas_call x6 -> x8, Pallas kernels: 153 us -> 234 us  [call(): pl.pallas_call(kernel, out_shape=out_shape, in_specs=specs, out_specs=jax...]
    ppermute x12 -> x8, starting transfers between devices: 39 us -> 25.3 us  [the longest x4 15.3 us: exchanged(): lax.ppermute(last, axis, forward)]
    ppermute x12 -> x8, waiting for transfers between devices: 15.9 us -> 4.96 us  [the longest x4 4.07 us: exchanged(): lax.ppermute(first, axis, backward)]
    ppermute x10, waiting for transfers between devices: 12.7 us -> 3.41 us  [joined(): other = lax.ppermute(stats, axis, [(i, i ^ step) for i in range(count)])]
    transpose x3 -> x0, local copies, waits for them, and re-layouts: 8.23 us -> none  [the longest x2 5.14 us: to_groups(): x = jnp.transpose(x, (1, 4, 2, 0, 3) + tuple(range(5, x.ndim)))]
    broadcast_in_dim x7 -> x2, local copies, waits for them, and re-layouts: 6.4 us -> 0.15 us  [rim(): live = jnp.repeat(mask_row, TILE)[None, :, None] > 0]
    reshape x7 -> x3, local copies, waits for them, and re-layouts: 7.05 us -> 1.53 us  [to_groups(): x = jnp.transpose(x.reshape(rows, cols // TILE, TILE, WIDTH), (1, 0, 2, 3))]
    select_n x10, other arithmetic: 4.53 us -> 0.8 us  [combine(): return jnp.where(row == HEAD, peak, out)]
  transfers between devices with their start and end apart: 22 -> 18, of which waited for: 10 -> 4; matrix products, arithmetic and copies ran while one was open for 8% -> 3% of each run, Pallas kernels for 24% -> 50%
where the time goes in v2:
time: 298 us; the launch traced here: 297 us
  Pallas kernels  234 us (79%)
  starting transfers between devices  38.4 us (13%)
  local copies, waits for them, and re-layouts  11.9 us (4%)
  waiting for transfers between devices  8.37 us (3%)
  other arithmetic  3.11 us (1%)
    pallas_call x8, Pallas kernels, call(): pl.pallas_call(kernel, out_shape=out_shape, in_specs=specs, out_specs=jax...  234 us
    ppermute x4, starting transfers between devices, exchanged(): lax.ppermute(last, axis, forward)  15.3 us
    ppermute x10, starting transfers between devices, joined(): other = lax.ppermute(stats, axis, [(i, i ^ step) for i in range(count)])  13.1 us
    ppermute x4, starting transfers between devices, exchanged(): lax.ppermute(first, axis, backward)  9.98 us
  transfers between devices with their start and end apart: 18, of which 4 were waited for; matrix products, arithmetic and copies ran while one was open for 3% of the time, Pallas kernels for 50%

profile of v2, /device:TPU:1, one launch (start us, length us, event | category | flops | bytes accessed | tf_op | source)
XLA Modules:
  0.0 297.4 jit_solution(16754358033796551469)
XLA Ops:
  3.5 4.7 %collective-permute-start = (bf16[1,6,48,256]{3,2,1,0:T(8,128)(2,1)}, bf16[1,6,48,256]{3,2,1,0:T(8,128)(2,1)}, u32[]{:S(2)}, u32[]{:S(2)}) collective-permute-start(bf16[1,6,48,256]{3,2,1,0:T(8,128)(2,1)} %bitcast.111), channel_id=1, source_target_pairs={{0,8},{8,16},{16,24},{1,9},{9,17},{17,25},{2,10},{10,18},{18,26},{... | collective-permute-start | bytes 442376 | tf_op jit(solution)/shard_map/ppermute | solution.py:573
  8.9 1.4 collective-permute-start.1
  11.4 5.5 %own_tokens.2 = (bf16[2304,256]{1,0:T(8,128)(2,1)S(1)}, bf16[2304,256]{1,0:T(8,128)(2,1)S(1)}, bf16[2304,256]{1,0:T(8,128)(2,1)S(1)}, bf16[2304,128]{1,0:T(8,128...) custom-call(bf16[2304,256]{1,0:T(8,128)(2,1)S(1)} %bitcast.112, ...), custom_call_target="tpu_custom_call" | custom-call | flops 6000000000 | bytes 6000000 | tf_op jit(solution)/shard_map/own_tokens/pallas_call | solution.py:451
  23.8 1.4 slice_bitcast_fusion.1
  25.7 1.2 collective-permute-start.5
  28.4 2.2 collective-permute-start.3
  30.8 1.3 collective-permute-start.6
  32.1 3.6 %collective-permute-start.2 = (bf16[1,480,256]{2,1,0:T(8,128)(2,1)S(1)}, bf16[1,480,256]{2,1,0:T(8,128)(2,1)S(1)}, u32[]{:S(2)}, u32[]{:S(2)}) collective-permute-start(bf16[1,480,256]{2,1,0:T(8,128)(2,1)S(1)} %pad_maximum_fusion.2), channel_id=1, source_target_pairs={{0,1},{1,2},{2,3},{3,4},{4,5},{5,6},{6,7},{8,9},{9,10},{10,11},{11... | collective-permute-start | bytes 737288 | tf_op jit(solution)/shard_map/ppermute | solution.py:573
  35.8 2.4 collective-permute-start.7
  38.2 66.6 %attend_middle.2.refs_19_ = bf16[1,4,384,256]{3,2,1,0:T(8,128)(2,1)S(1)} custom-call(s32[1,4]{1,0:T(1,128)S(1)} %add_convert_fusion.refs_0_, s32[6,6]{1,0:T(8,128)S(1)} %copy-done, bf16[1,6,384,256]{3,2,1,0:T(8,128)(2,1)S(1)} %get-tuple-element.59.refs_2_, bf16[1,6,384,256]{3,2,1,0:T(8,128)(2,1)S(1)} %bitcast.122, bf16[1,6,384,256]{3,2,1,0:T(8,128)(2,1)S(1)} %bitcast.124, ...), custom_call_target="tpu_custom_call" | custom-call | flops 12000000000 | bytes 12000000 | tf_op jit(solution)/shard_map/attend_middle/pallas_call | solution.py:451
  105.0 2.3 collective-permute-start.8
  107.3 38.0 %attend_edges.2 = (bf16[4,3,192,256]{3,2,1,0:T(8,128)(2,1)S(1)}, bf16[4,3,48,256]{3,2,1,0:T(8,128)(2,1)S(1)}, bf16[4,3,48,256]{3,2,1,0:T(8,128)(2,1)S(1)}) custom-call(s32[1,4]{1,0:T(1,128)S(1)} %add_convert_fusion.refs_0_, s32[6,6]{1,0:T(8,128)S(1)} %copy-done, bf16[1,6,384,256]{3,2,1,0:T(8,128)(2,1)S(1)} %get-tuple-element.59.refs_2_, ...), custom_call_target="tpu_custom_call" | custom-call | flops 12000000000 | bytes 12000000 | tf_op jit(solution)/shard_map/attend_edges/pallas_call | solution.py:451
  145.4 1.6 finish_registers.2.refs_2_.refs_9_.g_ref
  147.1 5.6 %own_tokens.3 = (bf16[2304,256]{1,0:T(8,128)(2,1)S(1)}, bf16[2304,256]{1,0:T(8,128)(2,1)S(1)}, bf16[2304,256]{1,0:T(8,128)(2,1)S(1)}, bf16[2304,128]{1,0:T(8,128...) custom-call(bf16[2304,256]{1,0:T(8,128)(2,1)S(1)} %bitcast.121, ...), custom_call_target="tpu_custom_call" | custom-call | flops 6000000000 | bytes 6000000 | tf_op jit(solution)/shard_map/own_tokens/pallas_call | solution.py:451
  154.3 3.3 %collective-permute-start.14 = (f32[40,512]{1,0:T(8,128)S(1)}, f32[40,512]{1,0:T(8,128)S(1)}, u32[]{:S(2)}, u32[]{:S(2)}) collective-permute-start(f32[40,512]{1,0:T(8,128)S(1)} %add_select_fusion.4), channel_id=1, source_target_pairs={{0,2},{1,3},{2,0},{3,1},{4,6},{5,7},{6,4},{7,5},{8,10},{9,11},{10,... | collective-permute-start | bytes 245768 | tf_op jit(solution)/shard_map/ppermute | solution.py:563
  157.6 2.5 collective-permute-done.14
  160.3 1.3 collective-permute-start.10
  161.6 4.0 %collective-permute-start.9 = (bf16[4,3,48,256]{3,2,0,1:T(8,128)(2,1)S(1)}, bf16[4,3,48,256]{3,2,0,1:T(8,128)(2,1)S(1)}, u32[]{:S(2)}, u32[]{:S(2)}) collective-permute-start(bf16[4,3,48,256]{3,2,0,1:T(8,128)(2,1)S(1)} %copy.16), channel_id=1, source_target_pairs={{0,8},{8,16},{16,24},{1,9},{9,17},{17,25},{2,10},{10,18},{18,26},{... | collective-permute-start | bytes 884744 | tf_op jit(solution)/shard_map/ppermute | solution.py:573
  165.7 4.1 %collective-permute-done.10 = bf16[4,3,48,256]{3,2,0,1:T(8,128)(2,1)S(1)} collective-permute-done((bf16[4,3,48,256]{3,2,0,1:T(8,128)(2,1)S(1)}, bf16[4,3,48,256]{3,2,0,1:T(8,128)(2,1)S(1)}, u32[]{:S(2)}, u32[]{:S(2)}) %collective-permute-start.10) | collective-permute-done | bytes 294944 | tf_op jit(solution)/shard_map/ppermute | solution.py:573
  170.8 5.1 %collective-permute-start.12 = (bf16[4,288,256]{2,1,0:T(8,128)(2,1)S(1)}, bf16[4,288,256]{2,1,0:T(8,128)(2,1)S(1)}, u32[]{:S(2)}, u32[]{:S(2)}) collective-permute-start(bf16[4,288,256]{2,1,0:T(8,128)(2,1)S(1)} %pad_maximum_fusion.1), channel_id=1, source_target_pairs={{1,0},{2,1},{3,2},{4,3},{5,4},{6,5},{7,6},{9,8},{10,9},{11,10},{12... | collective-permute-start | bytes 1769480 | tf_op jit(solution)/shard_map/ppermute | solution.py:573
  175.9 3.0 %collective-permute-start.11 = (bf16[4,288,256]{2,1,0:T(8,128)(2,1)S(1)}, bf16[4,288,256]{2,1,0:T(8,128)(2,1)S(1)}, u32[]{:S(2)}, u32[]{:S(2)}) collective-permute-start(bf16[4,288,256]{2,1,0:T(8,128)(2,1)S(1)} %pad_maximum_fusion), channel_id=1, source_target_pairs={{0,1},{1,2},{2,3},{3,4},{4,5},{5,6},{6,7},{8,9},{9,10},{10,11},{11... | collective-permute-start | bytes 1769480 | tf_op jit(solution)/shard_map/ppermute | solution.py:573
  180.1 37.0 %attend_middle.3.refs_19_ = bf16[4,1,192,256]{3,2,1,0:T(8,128)(2,1)S(1)} custom-call(s32[1,4]{1,0:T(1,128)S(1)} %add_convert_fusion.refs_0_, s32[6,6]{1,0:T(8,128)S(1)} %copy-done, bf16[4,3,192,256]{3,2,1,0:T(8,128)(2,1)S(1)} %get-tuple-element.25.refs_2_, bf16[4,3,192,256]{3,2,1,0:T(8,128)(2,1)S(1)} %bitcast.128, bf16[4,3,192,256]{3,2,1,0:T(8,128)(2,1)S(1)} %bitcast.130, ...), custom_call_target="tpu_custom_call" | custom-call | flops 12000000000 | bytes 12000000 | tf_op jit(solution)/shard_map/attend_middle/pallas_call | solution.py:451
  217.3 2.2 finish_registers.3
  219.6 77.8 %attend_edges.3 = bf16[48,48,256]{2,1,0:T(8,128)(2,1)} custom-call(s32[1,4]{1,0:T(1,128)S(1)} %add_convert_fusion.refs_0_, s32[6,6]{1,0:T(8,128)S(1)} %copy-done, bf16[4,3,192,256]{3,2,1,0:T(8,128)(2,1)S(1)} %get-tuple-element.25.refs_2_, bf16[4,3,192,256]{3,2,1,0:T(8,128)(2,1)S(1)} %bitcast.129, bf16[4,3,192,256]{3,2,1,0:T(8,128)(2,1)S(1)} %bitcast.131, ...), custom_call_target="tpu_custom_call" | custom-call | flops 12000000000 | bytes 12000000 | tf_op jit(solution)/shard_map/attend_edges/pallas_call | solution.py:451
  (111 shorter events, 18.1 us)
Async XLA Ops:
  0.6 9.7 %copy-start.10 = (bf16[48,48,256]{2,1,0:T(8,128)(2,1)S(1)}, bf16[48,48,256]{2,1,0:T(8,128)(2,1)}, u32[]{:S(2)}) copy-start(bf16[48,48,256]{2,1,0:T(8,128)(2,1)} %param.9) | copy-start | bytes 3538948
  3.5 23.4 %collective-permute-start = (bf16[1,6,48,256]{3,2,1,0:T(8,128)(2,1)}, bf16[1,6,48,256]{3,2,1,0:T(8,128)(2,1)}, u32[]{:S(2)}, u32[]{:S(2)}) collective-permute-start(bf16[1,6,48,256]{3,2,1,0:T(8,128)(2,1)} %bitcast.111), channel_id=1, source_target_pairs={{0,8},{8,16},{16,24},{1,9},{9,17},{17,25},{2,10},{10,18},{18,26},{... | collective-permute-start | bytes 442376 | tf_op jit(solution)/shard_map/ppermute | solution.py:573
  8.9 18.8 %collective-permute-start.1 = (bf16[1,6,48,256]{3,2,1,0:T(8,128)(2,1)}, bf16[1,6,48,256]{3,2,1,0:T(8,128)(2,1)}, u32[]{:S(2)}, u32[]{:S(2)}) collective-permute-start(bf16[1,6,48,256]{3,2,1,0:T(8,128)(2,1)} %bitcast.110), channel_id=1, source_target_pairs={{8,0},{16,8},{24,16},{9,1},{17,9},{25,17},{10,2},{18,10},{26,18},{... | collective-permute-start | bytes 442376 | tf_op jit(solution)/shard_map/ppermute | solution.py:573
  11.4 10.4 %copy-start.14 = (f32[2,256]{1,0:T(2,128)S(1)}, f32[2,256]{1,0:T(2,128)}, u32[]{:S(2)}) copy-start(f32[2,256]{1,0:T(2,128)} %param.17) | copy-start | bytes 6148
  20.9 4.7 %collective-permute-start.4 = (f32[40,512]{1,0:T(8,128)S(1)}, f32[40,512]{1,0:T(8,128)S(1)}, u32[]{:S(2)}, u32[]{:S(2)}) collective-permute-start(f32[40,512]{1,0:T(8,128)S(1)} %get-tuple-element.26), channel_id=1, source_target_pairs={{0,1},{1,0},{2,3},{3,2},{4,5},{5,4},{6,7},{7,6},{8,9},{9,8},{10,11... | collective-permute-start | bytes 245768 | tf_op jit(solution)/shard_map/ppermute | solution.py:563
  25.4 12.8 %copy-start.5 = (bf16[2304,256]{1,0:T(8,128)(2,1)S(1)}, bf16[2304,256]{1,0:T(8,128)(2,1)}, u32[]{:S(2)}) copy-start(bf16[2304,256]{1,0:T(8,128)(2,1)} %copy-done.4) | copy-start | bytes 3538948
  25.4 12.8 %copy-start.7 = (bf16[2304,256]{1,0:T(8,128)(2,1)S(1)}, bf16[2304,256]{1,0:T(8,128)(2,1)}, u32[]{:S(2)}) copy-start(bf16[2304,256]{1,0:T(8,128)(2,1)} %copy-done.6) | copy-start | bytes 3538948
  25.5 12.8 %copy-start.3 = (bf16[2304,256]{1,0:T(8,128)(2,1)S(1)}, bf16[2304,256]{1,0:T(8,128)(2,1)}, u32[]{:S(2)}) copy-start(bf16[2304,256]{1,0:T(8,128)(2,1)} %copy-done.2) | copy-start | bytes 3538948
  25.5 12.8 %copy-start.9 = (bf16[2304,128]{1,0:T(8,128)(2,1)S(1)}, bf16[2304,128]{1,0:T(8,128)(2,1)}, u32[]{:S(2)}) copy-start(bf16[2304,128]{1,0:T(8,128)(2,1)} %copy-done.8) | copy-start | bytes 1769476
  25.7 5.0 %collective-permute-start.5 = (f32[40,512]{1,0:T(8,128)S(1)}, f32[40,512]{1,0:T(8,128)S(1)}, u32[]{:S(2)}, u32[]{:S(2)}) collective-permute-start(f32[40,512]{1,0:T(8,128)S(1)} %add_select_fusion.9), channel_id=1, source_target_pairs={{0,2},{1,3},{2,0},{3,1},{4,6},{5,7},{6,4},{7,5},{8,10},{9,11},{10,... | collective-permute-start | bytes 245768 | tf_op jit(solution)/shard_map/ppermute | solution.py:563
  28.4 78.8 %collective-permute-start.3 = (bf16[1,480,256]{2,1,0:T(8,128)(2,1)S(1)}, bf16[1,480,256]{2,1,0:T(8,128)(2,1)S(1)}, u32[]{:S(2)}, u32[]{:S(2)}) collective-permute-start(bf16[1,480,256]{2,1,0:T(8,128)(2,1)S(1)} %pad_maximum_fusion.3), channel_id=1, source_target_pairs={{1,0},{2,1},{3,2},{4,3},{5,4},{6,5},{7,6},{9,8},{10,9},{11,10},{12... | collective-permute-start | bytes 737288 | tf_op jit(solution)/shard_map/ppermute | solution.py:573
  30.8 4.9 %collective-permute-start.6 = (f32[40,512]{1,0:T(8,128)S(1)}, f32[40,512]{1,0:T(8,128)S(1)}, u32[]{:S(2)}, u32[]{:S(2)}) collective-permute-start(f32[40,512]{1,0:T(8,128)S(1)} %add_select_fusion.8), channel_id=1, source_target_pairs={{0,4},{1,5},{2,6},{3,7},{4,0},{5,1},{6,2},{7,3},{8,12},{9,13},{10,... | collective-permute-start | bytes 245768 | tf_op jit(solution)/shard_map/ppermute | solution.py:563
  32.1 75.2 %collective-permute-start.2 = (bf16[1,480,256]{2,1,0:T(8,128)(2,1)S(1)}, bf16[1,480,256]{2,1,0:T(8,128)(2,1)S(1)}, u32[]{:S(2)}, u32[]{:S(2)}) collective-permute-start(bf16[1,480,256]{2,1,0:T(8,128)(2,1)S(1)} %pad_maximum_fusion.2), channel_id=1, source_target_pairs={{0,1},{1,2},{2,3},{3,4},{4,5},{5,6},{6,7},{8,9},{9,10},{10,11},{11... | collective-permute-start | bytes 737288 | tf_op jit(solution)/shard_map/ppermute | solution.py:573
  35.8 69.0 %collective-permute-start.7 = (f32[40,512]{1,0:T(8,128)S(1)}, f32[40,512]{1,0:T(8,128)S(1)}, u32[]{:S(2)}, u32[]{:S(2)}) collective-permute-start(f32[40,512]{1,0:T(8,128)S(1)} %add_select_fusion.7), channel_id=1, source_target_pairs={{0,8},{8,0},{16,24},{24,16},{1,9},{9,1},{17,25},{25,17},{2,10},{10... | collective-permute-start | bytes 245768 | tf_op jit(solution)/shard_map/ppermute | solution.py:563
  105.0 40.3 %collective-permute-start.8 = (f32[40,512]{1,0:T(8,128)S(1)}, f32[40,512]{1,0:T(8,128)S(1)}, u32[]{:S(2)}, u32[]{:S(2)}) collective-permute-start(f32[40,512]{1,0:T(8,128)S(1)} %add_select_fusion.6), channel_id=1, source_target_pairs={{0,16},{8,24},{16,0},{24,8},{1,17},{9,25},{17,1},{25,9},{2,18},{10... | collective-permute-start | bytes 245768 | tf_op jit(solution)/shard_map/ppermute | solution.py:563
  152.7 1.5 collective-permute-start.13
  154.3 5.8 %collective-permute-start.14 = (f32[40,512]{1,0:T(8,128)S(1)}, f32[40,512]{1,0:T(8,128)S(1)}, u32[]{:S(2)}, u32[]{:S(2)}) collective-permute-start(f32[40,512]{1,0:T(8,128)S(1)} %add_select_fusion.4), channel_id=1, source_target_pairs={{0,2},{1,3},{2,0},{3,1},{4,6},{5,7},{6,4},{7,5},{8,10},{9,11},{10,... | collective-permute-start | bytes 245768 | tf_op jit(solution)/shard_map/ppermute | solution.py:563
  160.2 5.4 %collective-permute-start.15 = (f32[40,512]{1,0:T(8,128)S(1)}, f32[40,512]{1,0:T(8,128)S(1)}, u32[]{:S(2)}, u32[]{:S(2)}) collective-permute-start(f32[40,512]{1,0:T(8,128)S(1)} %add_select_fusion.3), channel_id=1, source_target_pairs={{0,4},{1,5},{2,6},{3,7},{4,0},{5,1},{6,2},{7,3},{8,12},{9,13},{10,... | collective-permute-start | bytes 245768 | tf_op jit(solution)/shard_map/ppermute | solution.py:563
  160.3 9.5 %collective-permute-start.10 = (bf16[4,3,48,256]{3,2,0,1:T(8,128)(2,1)S(1)}, bf16[4,3,48,256]{3,2,0,1:T(8,128)(2,1)S(1)}, u32[]{:S(2)}, u32[]{:S(2)}) collective-permute-start(bf16[4,3,48,256]{3,2,0,1:T(8,128)(2,1)S(1)} %copy.17), channel_id=1, source_target_pairs={{8,0},{16,8},{24,16},{9,1},{17,9},{25,17},{10,2},{18,10},{26,18},{... | collective-permute-start | bytes 884744 | tf_op jit(solution)/shard_map/ppermute | solution.py:573
  161.6 9.1 %collective-permute-start.9 = (bf16[4,3,48,256]{3,2,0,1:T(8,128)(2,1)S(1)}, bf16[4,3,48,256]{3,2,0,1:T(8,128)(2,1)S(1)}, u32[]{:S(2)}, u32[]{:S(2)}) collective-permute-start(bf16[4,3,48,256]{3,2,0,1:T(8,128)(2,1)S(1)} %copy.16), channel_id=1, source_target_pairs={{0,8},{8,16},{16,24},{1,9},{9,17},{17,25},{2,10},{10,18},{18,26},{... | collective-permute-start | bytes 884744 | tf_op jit(solution)/shard_map/ppermute | solution.py:573
  165.7 13.2 %collective-permute-start.16 = (f32[40,512]{1,0:T(8,128)S(1)}, f32[40,512]{1,0:T(8,128)S(1)}, u32[]{:S(2)}, u32[]{:S(2)}) collective-permute-start(f32[40,512]{1,0:T(8,128)S(1)} %add_select_fusion.2), channel_id=1, source_target_pairs={{0,8},{8,0},{16,24},{24,16},{1,9},{9,1},{17,25},{25,17},{2,10},{10... | collective-permute-start | bytes 245768 | tf_op jit(solution)/shard_map/ppermute | solution.py:563
  170.8 48.8 %collective-permute-start.12 = (bf16[4,288,256]{2,1,0:T(8,128)(2,1)S(1)}, bf16[4,288,256]{2,1,0:T(8,128)(2,1)S(1)}, u32[]{:S(2)}, u32[]{:S(2)}) collective-permute-start(bf16[4,288,256]{2,1,0:T(8,128)(2,1)S(1)} %pad_maximum_fusion.1), channel_id=1, source_target_pairs={{1,0},{2,1},{3,2},{4,3},{5,4},{6,5},{7,6},{9,8},{10,9},{11,10},{12... | collective-permute-start | bytes 1769480 | tf_op jit(solution)/shard_map/ppermute | solution.py:573
  175.9 43.7 %collective-permute-start.11 = (bf16[4,288,256]{2,1,0:T(8,128)(2,1)S(1)}, bf16[4,288,256]{2,1,0:T(8,128)(2,1)S(1)}, u32[]{:S(2)}, u32[]{:S(2)}) collective-permute-start(bf16[4,288,256]{2,1,0:T(8,128)(2,1)S(1)} %pad_maximum_fusion), channel_id=1, source_target_pairs={{0,1},{1,2},{2,3},{3,4},{4,5},{5,6},{6,7},{8,9},{9,10},{10,11},{11... | collective-permute-start | bytes 1769480 | tf_op jit(solution)/shard_map/ppermute | solution.py:573
  179.1 38.1 %collective-permute-start.17 = (f32[40,512]{1,0:T(8,128)S(1)}, f32[40,512]{1,0:T(8,128)S(1)}, u32[]{:S(2)}, u32[]{:S(2)}) collective-permute-start(f32[40,512]{1,0:T(8,128)S(1)} %add_select_fusion.1), channel_id=1, source_target_pairs={{0,16},{8,24},{16,0},{24,8},{1,17},{9,25},{17,1},{25,9},{2,18},{10... | collective-permute-start | bytes 245768 | tf_op jit(solution)/shard_map/ppermute | solution.py:563
  (9 other events, 10.5 us)
